TPU v7x, 32 devices: a whole 2x2x4 slice. The times are simulated.
32 devices in a mesh: groups: 2 (over y), mom: 4 (over z), tm: 4 (over x, core).
Axes of the slice: x: 2, y: 2, z: 4, core: 2. Of those that a mesh axis runs over, the one named last changes fastest.
Arguments:
- panel_start: float32 [256, 4, 64, 512], P('mom', 'groups', None, 'tm'), parts along dimension 1, may hold values from -6 to 6
- block_guess: float32 [256, 4, 64, 128], P('mom', 'groups', 'tm'), parts along dimension 1, may hold values from -6 to 6
- coupling: float32 [2], P('groups'), parts along dimension 0, may hold values from 0.3 to 0.6
- slab_owner: int32 [8], P('groups'), parts along dimension 0, may hold values from 0 to 3, each once
- expiring: int32 [2], P('groups'), parts along dimension 0, may hold values from 0 to 3
- ordering: int32 [256], replicated, may hold values from 0 to 255, each once
Outputs:
- history_out: float32 [256, 4, 64, 512], P('mom', 'groups', None, 'tm'), parts along dimension 1
There are 2 independent parts, one for each index of `groups`. A program takes and returns all parts, laid end to end along the dimension named above; an argument that names none is the same for every part. Nothing has to cross between parts.
Inputs may be any that keep to these rules, and one draw needn't show every extreme that they name: `slab_owner`: entry s is the column block that holds history slab s; each block once. `ordering`: entry j is qx * 16 + qy for the momentum of stored row j; each momentum once.
All inputs are finite; a program needn't handle non-finite values.
Results may differ from a plain program's by a relative error of at most 0.0001.
Values sent between devices are 32-bit elements; how exact they have to be, the bound alone decides.
A program may use at most 128 MiB of HBM per device.

v0:
```python
import functools
import math

import jax
import jax.numpy as jnp
from jax import lax
from jax.experimental import pallas as pl
from jax.experimental.pallas import tpu as pltpu
from jax.sharding import PartitionSpec as P

LSIDE = 16
K = LSIDE * LSIDE
PANEL = 64
PASSES = 2
SPIN = 2
LANES = 2 * PANEL
CHUNKS = 2
MESH = pl.DeviceIdType.MESH


def tables(ordering):
    bits = LSIDE.bit_length() - 1
    site = lax.broadcasted_iota(jnp.int32, (K, K), 0)
    phases = ((site >> bits) * (ordering >> bits) + (site & (LSIDE - 1)) * (ordering & (LSIDE - 1))) & (LSIDE - 1)
    angles = phases.astype(jnp.float32) * (2.0 * math.pi / LSIDE)
    return jnp.cos(angles) / LSIDE, jnp.sin(angles) / LSIDE


def split(x):
    high = x.astype(jnp.bfloat16)
    return high, (x - high.astype(jnp.float32)).astype(jnp.bfloat16)


def dot3(left, right, transposed=False):
    dims = (((1,), (1 if transposed else 0,)), ((), ()))

    def one(a, b):
        return lax.dot_general(a, b, dims, preferred_element_type=jnp.float32)

    return one(left[0], right[0]) + (one(left[0], right[1]) + one(left[1], right[0]))


def step_kernel(
    n_mom, n_tm, start, guess, ordering, wvec, chosen,
    out, cur, recv, sig, ret, fwd_split, back_split, stk, part, conv, pair_buf, ring_buf, guess_all,
    local_sem, guess_own, fs, fr, rs, rr, ps, pr, ss, sr, gs, gr, qs, qr, ds, dr,
):
    mom, tm = lax.axis_index("mom"), lax.axis_index("tm")
    rows, local_k = cur.shape[3], cur.shape[4]
    group = n_mom * rows
    n_x = n_tm // 2
    half = local_k // 2
    share = half // n_x
    tm_x, core = tm // 2, tm % 2
    step_scale = 1.0 / math.sqrt(PANEL)
    lane = lax.broadcasted_iota(jnp.int32, (1, LANES), 1)
    low = lane < PANEL
    sign = jnp.where(low, -1.0, 1.0).astype(jnp.float32)
    flat_cur = cur.reshape(CHUNKS * SPIN * group * local_k, LANES)
    flat_ret = ret.reshape(CHUNKS * SPIN * group * local_k, LANES)

    def swap(x):
        return pltpu.roll(x, PANEL, 1)

    def rot(x):
        return swap(x) * sign

    barrier = pltpu.get_barrier_semaphore()
    for o in range(1, n_mom):
        pl.semaphore_signal(barrier, inc=1, device_id={"mom": lax.rem(mom + o, n_mom)}, device_id_type=MESH)
    for o in range(1, n_tm):
        pl.semaphore_signal(barrier, inc=1, device_id={"tm": lax.rem(tm + o, n_tm)}, device_id_type=MESH)

    mine = pl.ds(mom * local_k, local_k)
    other_half = pl.ds((1 - core) * half, half)
    share_at = core * half + tm_x * share
    own_share = pl.ds(share_at, share)
    partner = {"tm": tm_x * 2 + (1 - core)}

    def remote(source, target, send, recv_sem, device):
        return pltpu.make_async_remote_copy(
            src_ref=source, dst_ref=target, send_sem=send, recv_sem=recv_sem,
            device_id=device, device_id_type=MESH)

    def forward(n, c, o):
        peer = lax.rem(mom + o, n_mom)
        return remote(cur.at[c, :, peer], recv.at[c, :, :, mine, :], fs.at[n, c, o], fr.at[n, c, o], {"mom": peer})

    def forward_own(n, c):
        return pltpu.make_async_copy(cur.at[c, :, mom], recv.at[c, :, :, mine, :], local_sem.at[n, c, 0])

    def back(n, c, o):
        peer = lax.rem(mom + o, n_mom)
        return remote(
            sig.at[c, :, :, pl.ds(peer * local_k, local_k), :], ret.at[c, :, mom],
            rs.at[n, c, o], rr.at[n, c, o], {"mom": peer})

    def back_own(n, c):
        return pltpu.make_async_copy(sig.at[c, :, :, mine, :], ret.at[c, :, mom], local_sem.at[n, c, 1])

    def pair_up(n, c):
        return remote(part.at[c, other_half], pair_buf.at[c], ps.at[n, c], pr.at[n, c], partner)

    def scatter(n, c, o):
        peer = lax.rem(tm_x + o, n_x)
        return remote(
            part.at[c, pl.ds(core * half + peer * share, share)], ring_buf.at[c, o - 1],
            ss.at[n, c, o], sr.at[n, c, o], {"tm": peer * 2 + core})

    def gather(n, c, o):
        peer = lax.rem(tm_x + o, n_x)
        return remote(
            conv.at[c, own_share], conv.at[c, own_share],
            gs.at[n, c, o], gr.at[n, c, o], {"tm": peer * 2 + core})

    def pair_down(n, c, o):
        held = pl.ds(core * half + lax.rem(tm_x + n_x - o, n_x) * share, share)
        return remote(conv.at[c, held], conv.at[c, held], qs.at[n, c, o], qr.at[n, c, o], partner)

    def pair_down_recv(n, c):
        for o in range(n_x):
            pair_down(n, c, o).wait_recv()

    def guess_copy(o):
        return remote(guess, guess_all.at[tm], ds.at[o], dr.at[o], {"tm": lax.rem(tm + o, n_tm)})

    def guess_local():
        return pltpu.make_async_copy(guess, guess_all.at[tm], guess_own)

    def send_forward(n, c):
        for o in range(1, n_mom):
            forward(n, c, o).start()
        forward_own(n, c).start()

    def keep_stack(n, k, s, c, value):
        turned = rot(value)
        for at, piece in ((c * group, value), (PANEL + c * group, turned)):
            high, rest = split(piece)
            stk[n, 0, k, s, at:at + group, :] = high
            stk[n, 1, k, s, at:at + group, :] = rest

    def first_layout(c):
        @pl.loop(0, local_k)
        def _(k):
            for s in range(SPIN):
                at = ((c * SPIN + s) * group) * local_k + k
                flat_cur[pl.ds(at, group, stride=local_k), :] = start[k, s, c]

    def sigma(n, c):
        for o in range(1, n_mom):
            forward(n, c, o).wait_recv()
        forward_own(n, c).wait()
        if n > 0:
            for o in range(1, n_mom):
                back(n - 1, c, o).wait_send()

        @pl.loop(0, rows)
        def _(i):
            both = jnp.concatenate([recv[c, 0, i], recv[c, 1, i]], axis=1)
            sums = dot3((fwd_split[0], fwd_split[1]), split(both))
            site, mirrored = [], []
            for s in range(SPIN):
                with_cos = sums[:K, s * LANES:(s + 1) * LANES]
                turned = rot(sums[K:, s * LANES:(s + 1) * LANES])
                site.append(with_cos + turned)
                mirrored.append(with_cos - turned)
            first, second = site
            flipped = swap(second)
            pair = (first * jnp.where(low, second, flipped)
                    + rot(first) * jnp.where(low, flipped, second)) * wvec[...]
            pair_rot = rot(pair)
            tops, bottoms = [], []
            for s in range(SPIN):
                other = mirrored[1 - s]
                flipped = swap(other)
                value = pair * jnp.where(low, other, flipped) - pair_rot * jnp.where(low, flipped, other)
                tops.append(value)
                bottoms.append(-rot(value))
            stacked = jnp.concatenate(
                [jnp.concatenate(tops, axis=1), jnp.concatenate(bottoms, axis=1)], axis=0)
            result = dot3((back_split[0], back_split[1]), split(stacked))
            for s in range(SPIN):
                sig[c, s, i] = result[:, s * LANES:(s + 1) * LANES]

        for o in range(1, n_mom):
            back(n, c, o).start()
        back_own(n, c).start()

    def convolve(n, c):
        for o in range(1, n_mom):
            back(n, c, o).wait_recv()
        back_own(n, c).wait()
        if n > 0:
            pair_up(n - 1, c).wait_send()
            for o in range(n_x):
                pair_down(n - 1, c, o).wait_send()
            for o in range(1, n_x):
                scatter(n - 1, c, o).wait_send()
                gather(n - 1, c, o).wait_send()

        def some(base):
            @pl.loop(0, half, unroll=8)
            def _(i):
                k = base + i
                for s in range(SPIN):
                    at = ((c * SPIN + s) * group) * local_k + k
                    value = split(flat_ret[pl.ds(at, group, stride=local_k), :])
                    part[c, k, s] = dot3(value, (stk[n, 0, k, s], stk[n, 1, k, s]), True)

        some((1 - core) * half)
        pair_up(n, c).start()
        some(core * half)

    def reduce(n, c):
        pair_up(n, c).wait_recv()

        @pl.loop(0, half)
        def _(i):
            part[c, core * half + i] = part[c, core * half + i] + pair_buf[c, i]

        for o in range(1, n_x):
            scatter(n, c, o).start()
        for o in range(1, n_x):
            scatter(n, c, o).wait_recv()

        @pl.loop(0, share)
        def _(i):
            total = part[c, share_at + i]
            for o in range(1, n_x):
                total = total + ring_buf[c, o - 1, i]
            conv[c, share_at + i] = total

        for o in range(1, n_x):
            gather(n, c, o).start()
        pair_down(n, c, 0).start()
        for o in range(1, n_x):
            gather(n, c, o).wait_recv()
            pair_down(n, c, o).start()

    def update(n, c):
        for o in range(1, n_mom):
            forward(n, c, o).wait_send()

        def some(base):
            @pl.loop(0, half, unroll=8)
            def _(i):
                k = base + i
                for s in range(SPIN):
                    new = start[k, s, c] + step_scale * dot3(
                        split(conv[c, k, s]), (stk[n, 0, k, s], stk[n, 1, k, s]))
                    at = ((c * SPIN + s) * group) * local_k + k
                    flat_cur[pl.ds(at, group, stride=local_k), :] = new
                    keep_stack(n + 1, k, s, c, new)

        some(core * half)
        pair_down_recv(n, c)
        some((1 - core) * half)

    def finish(n):
        is_block = chosen[...] > 0.5

        def some(base):
            @pl.loop(0, half, unroll=4)
            def _(i):
                k = base + i
                for s in range(SPIN):
                    whole = jnp.concatenate([conv[c, k, s] for c in range(CHUNKS)], axis=0)
                    d = jnp.concatenate([guess_all[t, k, s] for t in range(n_tm)], axis=0)
                    first = jnp.concatenate([start[k, s, c] for c in range(CHUNKS)], axis=0)
                    panel = stk[n, 0, k, s].astype(jnp.float32) + stk[n, 1, k, s].astype(jnp.float32)
                    right = jnp.where(is_block, jnp.concatenate([whole, rot(whole)], axis=0), panel)
                    left = jnp.where(is_block, d, whole)
                    new = jnp.where(is_block, d, first) + step_scale * dot3(split(left), split(right))
                    for c in range(CHUNKS):
                        out[k, s, c] = new[c * group:(c + 1) * group, :]

        for c in range(CHUNKS - 1):
            pair_down_recv(n, c)
        some(core * half)
        pair_down_recv(n, CHUNKS - 1)
        some((1 - core) * half)

    first_layout(0)
    pl.semaphore_wait(barrier, n_mom + n_tm - 2)
    send_forward(0, 0)
    for c in range(1, CHUNKS):
        first_layout(c)
        send_forward(0, c)
    for o in range(1, n_tm):
        guess_copy(o).start()
    guess_local().start()

    for at, table in enumerate(tables(ordering[...])):
        fwd_split[0, at * K:(at + 1) * K, :], fwd_split[1, at * K:(at + 1) * K, :] = split(table)
        turned = split(table.T)
        back_split[0, :, at * K:(at + 1) * K], back_split[1, :, at * K:(at + 1) * K] = turned

    @pl.loop(0, local_k, unroll=4)
    def _(k):
        for s in range(SPIN):
            for c in range(CHUNKS):
                keep_stack(0, k, s, c, start[k, s, c])

    for n in range(PASSES):
        for c in range(CHUNKS):
            sigma(n, c)
        for c in range(CHUNKS):
            convolve(n, c)
            reduce(n, c)
            if n < PASSES - 1:
                update(n, c)
                send_forward(n + 1, c)

    for o in range(1, n_tm):
        guess_copy(o).wait_recv()
    guess_local().wait()
    finish(PASSES - 1)

    n = PASSES - 1
    for c in range(CHUNKS):
        pair_up(n, c).wait_send()
        for o in range(n_x):
            pair_down(n, c, o).wait_send()
        for o in range(1, n_x):
            scatter(n, c, o).wait_send()
            gather(n, c, o).wait_send()
        for o in range(1, n_mom):
            forward(n, c, o).wait_send()
            back(n, c, o).wait_send()
    for o in range(1, n_tm):
        guess_copy(o).wait_send()


def panel_step(n_mom, n_tm, start, guess, ordering, wvec, chosen):
    local_k = start.shape[0]
    group = start.shape[3]
    rows = group // n_mom
    share = local_k // n_tm
    panel = (CHUNKS, SPIN, n_mom, rows, local_k, LANES)
    sites = (CHUNKS, SPIN, rows, K, LANES)
    f32, bf16 = jnp.float32, jnp.bfloat16
    dma = pltpu.SemaphoreType.DMA
    vmem = pl.BlockSpec(memory_space=pltpu.VMEM)
    one, many_mom, many_x = (PASSES, CHUNKS), (PASSES, CHUNKS, n_mom), (PASSES, CHUNKS, n_tm // 2)
    return pl.pallas_call(
        functools.partial(step_kernel, n_mom, n_tm),
        out_shape=jax.ShapeDtypeStruct(start.shape, f32),
        in_specs=[vmem] * 5,
        out_specs=vmem,
        scratch_shapes=[
            pltpu.VMEM(panel, f32),
            pltpu.VMEM(sites, f32),
            pltpu.VMEM(sites, f32),
            pltpu.VMEM(panel, f32),
            pltpu.VMEM((2, 2 * K, K), bf16),
            pltpu.VMEM((2, K, 2 * K), bf16),
            pltpu.VMEM((PASSES, 2, local_k, SPIN, LANES, LANES), bf16),
            pltpu.VMEM((CHUNKS, local_k, SPIN, group, LANES), f32),
            pltpu.VMEM((CHUNKS, local_k, SPIN, group, LANES), f32),
            pltpu.VMEM((CHUNKS, local_k // 2, SPIN, group, LANES), f32),
            pltpu.VMEM((CHUNKS, max(n_tm // 2 - 1, 1), share, SPIN, group, LANES), f32),
            pltpu.VMEM((n_tm,) + guess.shape, f32),
            dma(one + (2,)), dma,
            dma(many_mom), dma(many_mom), dma(many_mom), dma(many_mom),
            dma(one), dma(one),
            dma(many_x), dma(many_x), dma(many_x), dma(many_x),
            dma(many_x), dma(many_x),
            dma((n_tm,)), dma((n_tm,)),
        ],
        compiler_params=pltpu.CompilerParams(
            collective_id=0, has_side_effects=True, vmem_limit_bytes=63 * 1024 * 1024),
        name="panel_step",
    )(start, guess, ordering, wvec, chosen)


def body(panel_start, block_guess, coupling, slab_owner, expiring, ordering):
    slab_count = lax.axis_size("tm")
    n_mom = lax.axis_size("mom")
    own_index = lax.axis_index("tm")
    blocks = jnp.arange(slab_count, dtype=jnp.int32)
    slab_mine = jnp.sum(blocks * (slab_owner == own_index).astype(jnp.int32))
    position = (slab_mine - expiring[0]) % slab_count
    window = slab_count * PANEL
    times = position * PANEL + jnp.arange(PANEL, dtype=jnp.int32)
    weights = jnp.exp(-1.5 * (window - 1 - times).astype(jnp.float32) / window) / math.sqrt(window)
    strength = coupling[0] * coupling[0]
    wvec = (strength * jnp.concatenate([weights, weights]))[None, :]
    owner_expiring = jnp.sum(slab_owner * (blocks == expiring[0]).astype(jnp.int32))
    chosen = jnp.broadcast_to((own_index == owner_expiring).astype(jnp.float32), (1, LANES))
    local_k = panel_start.shape[0]
    start = panel_start.reshape(local_k, SPIN, CHUNKS, PANEL // CHUNKS, LANES)
    result = panel_step(n_mom, slab_count, start, block_guess, ordering[None, :], wvec, chosen)
    return result.reshape(panel_start.shape)


def solution(mesh):
    return jax.shard_map(
        body,
        mesh=mesh,
        in_specs=(
            P("mom", "groups", None, "tm"),
            P("mom", "groups", "tm", None),
            P("groups"),
            P("groups"),
            P("groups"),
            P(),
        ),
        out_specs=P("mom", "groups", None, "tm"),
        check_vma=False,
    )
```

profile of v0, /device:TPU:28, one launch (start us, length us, event | category | flops | bytes accessed | tf_op | source)
XLA Modules:
  0.0 426.8 jit_solution(13235028879318406661)
XLA Ops:
  1.3 1.3 fusion.1
  3.8 0.5 broadcast_in_dim.8.chosen
  4.4 0.6 maximum_multiply_fusion.wvec
  5.0 417.1 %panel_step.1 = f32[64,2,2,32,128]{4,3,2,1,0:T(8,128)} custom-call(f32[64,2,2,32,128]{4,3,2,1,0:T(8,128)} %bitcast.10, f32[64,2,16,128]{3,2,1,0:T(8,128)} %guess.1, s32[1,256]{1,0:T(1,128)} %bitcast.11, f32[1,128]{1,0:T(1,128)} %maximum_multiply_fusion.wvec, f32[1,128]{1,0:T(1,128)} %broadcast_in_dim.8.chosen), custom_call_target="tpu_custom_call" | custom-call | tf_op jit(solution)/shard_map/panel_step/pallas_call | solution.py:345
  422.0 4.8 %copy.10 = f32[64,2,64,128]{3,2,1,0:T(8,128)} copy(f32[64,2,64,128]{3,2,1,0:T(8,128)} %bitcast.9) | data formatting | bytes 8388608
  (1 shorter events, 0.0 us)
where the time goes:
time: 427 us
  Pallas kernels  417 us (98%)
  local copies, waits for them, and re-layouts  5.31 us (1%)
    pallas_call x1, Pallas kernels, panel_step(): pl.pallas_call(functools.partial(step_kernel, n_mom, n_tm), out_shape=jax...  417 us

commit v1 on v0

--- a/solution.py
+++ b/solution.py
@@ -373,6 +373,682 @@
     )(start, guess, ordering, wvec, chosen)
 
 
+SUBLANES = 8
+CHUNK = 2
+LAG = 2
+LEAD = 2
+
+
+def block_transpose(blocks, lane, width):
+    blocks = list(blocks)
+    bit = 1
+    while bit < len(blocks):
+        keep = (lane // width) % (2 * bit) < bit
+        for p in range(len(blocks)):
+            if p & bit == 0:
+                a, b = blocks[p], blocks[p + bit]
+                blocks[p] = jnp.where(keep, a, pltpu.roll(b, bit * width, 1))
+                blocks[p + bit] = jnp.where(keep, pltpu.roll(a, LANES - bit * width, 1), b)
+        bit *= 2
+    return blocks
+
+
+def share_kernel(
+    n, start, guess, ordering, wvec, chosen,
+    out, snd, recv, sig, rx_g, rx_s, stk, rbuf, lbuf, tot, guess_all, fwd_split, back_split,
+    fl, fs, fr, gl, gs, gr, sl, ss, sr, tl, ts, tr, rs, rr, ls, lr, credit, room, cl, cs, cr,
+    al, aps, apr, axs, axr, aqs, aqr,
+):
+    mom, tm = lax.axis_index("mom"), lax.axis_index("tm")
+    local_k = start.shape[0]
+    quarter = local_k // n
+    rows = PANEL // n
+    width = PANEL // n
+    halves = rows // SUBLANES
+    half_rows = n * SUBLANES
+    subs = quarter // SUBLANES
+    per_half = n * subs
+    pieces = halves * per_half
+    chunks = rows // CHUNK
+    half_chunks = SUBLANES // CHUNK
+    n_x = n // 2
+    tm_x, core = tm // 2, tm % 2
+    partner = {"tm": tm_x * 2 + (1 - core)}
+    step_scale = 1.0 / math.sqrt(PANEL)
+    lane = lax.broadcasted_iota(jnp.int32, (1, LANES), 1)
+    low = lane < PANEL
+    sign = jnp.where(low, -1.0, 1.0).astype(jnp.float32)
+    flat = n * rows * SPIN * local_k
+    flat_snd = snd.reshape(flat, LANES)
+    flat_recv = recv.reshape(flat, LANES)
+    flat_sig = sig.reshape(flat, LANES)
+    flat_rx_g = rx_g.reshape(flat, LANES)
+    flat_rx_s = rx_s.reshape(flat, LANES)
+    own_first = rx_g.reshape(local_k, SPIN, PANEL, LANES)
+    own_last = recv.reshape(halves, local_k, SPIN, half_rows, LANES)
+    near_left = mom < n // 2
+
+    def swap(x):
+        return pltpu.roll(x, PANEL, 1)
+
+    def rot(x):
+        return swap(x) * sign
+
+    barrier = pltpu.get_barrier_semaphore()
+    for o in range(1, n):
+        pl.semaphore_signal(barrier, inc=1, device_id={"mom": lax.rem(mom + o, n)}, device_id_type=MESH)
+    for o in range(1, n):
+        pl.semaphore_signal(barrier, inc=1, device_id={"tm": lax.rem(tm + o, n)}, device_id_type=MESH)
+
+    def remote(source, target, send, recv_sem, device):
+        return pltpu.make_async_remote_copy(
+            src_ref=source, dst_ref=target, send_sem=send, recv_sem=recv_sem,
+            device_id=device, device_id_type=MESH)
+
+    def local(source, target, sem):
+        return pltpu.make_async_copy(source, target, sem)
+
+    def span(q):
+        return pl.ds(q * CHUNK, CHUNK)
+
+    def forward(q, o):
+        peer = lax.rem(mom + o, n)
+        return remote(snd.at[peer, span(q)], recv.at[span(q), :, mom], fs.at[q, o], fr.at[q, o], {"mom": peer})
+
+    def forward_own(q):
+        return local(snd.at[mom, span(q)], recv.at[span(q), :, mom], fl.at[q])
+
+    def panel_out(q, o):
+        peer = lax.rem(tm + o, n)
+        return remote(recv.at[span(q), :, :, peer], rx_g.at[tm, span(q)], gs.at[q, o], gr.at[q, o], {"tm": peer})
+
+    def panel_own(q):
+        return local(recv.at[span(q), :, :, tm], rx_g.at[tm, span(q)], gl.at[q])
+
+    def sigma_out(n_pass, q, o):
+        peer = lax.rem(tm + o, n)
+        return remote(
+            sig.at[span(q), :, :, peer], rx_s.at[tm, span(q)], ss.at[n_pass, q, o], sr.at[n_pass, q, o], {"tm": peer})
+
+    def sigma_own(n_pass, q):
+        return local(sig.at[span(q), :, :, tm], rx_s.at[tm, span(q)], sl.at[n_pass, q])
+
+    def place(p):
+        half, rest = p // per_half, p % per_half
+        sub, turn = rest // n, rest % n
+        odd = turn % 2
+        block = (1 - odd) * (n - 1 - turn // 2) + odd * (turn // 2)
+        return half, sub, block
+
+    def next_out(p, o):
+        half, sub, block = place(p)
+        peer = lax.rem(tm + o, n)
+        at, ks = pl.ds(half * SUBLANES, SUBLANES), pl.ds(sub * SUBLANES, SUBLANES)
+        return remote(
+            snd.at[peer, at, :, block, ks], recv.at[at, :, block, tm, ks], ts.at[p, o], tr.at[p, o], {"tm": peer})
+
+    def next_own(p):
+        half, sub, block = place(p)
+        at, ks = pl.ds(half * SUBLANES, SUBLANES), pl.ds(sub * SUBLANES, SUBLANES)
+        return local(snd.at[tm, at, :, block, ks], recv.at[at, :, block, tm, ks], tl.at[p])
+
+    def window(p):
+        half, sub, block = place(p)
+        return pl.ds(block * quarter + sub * SUBLANES, SUBLANES), pl.ds(half * half_rows, half_rows)
+
+    def right_out(n_pass, p):
+        ks, at = window(p)
+        return remote(
+            rbuf.at[ks, :, at], rbuf.at[ks, :, at], rs.at[n_pass, p], rr.at[n_pass, p],
+            {"mom": jnp.minimum(mom + 1, n - 1)})
+
+    def left_out(n_pass, p):
+        ks, at = window(p)
+        return remote(
+            lbuf.at[ks, :, at], lbuf.at[ks, :, at], ls.at[n_pass, p], lr.at[n_pass, p],
+            {"mom": jnp.maximum(mom - 1, 0)})
+
+    def last_out(half, sub, o):
+        at = half * subs + sub
+        return remote(
+            tot.at[1, pl.ds(sub * SUBLANES, SUBLANES), :, pl.ds(half * half_rows, half_rows)],
+            own_last.at[half, pl.ds(tm * quarter + sub * SUBLANES, SUBLANES)],
+            cs.at[at, o], cr.at[at, o], {"tm": lax.rem(tm + o, n)})
+
+    def last_own(half, sub):
+        return local(
+            tot.at[1, pl.ds(sub * SUBLANES, SUBLANES), :, pl.ds(half * half_rows, half_rows)],
+            own_last.at[half, pl.ds(tm * quarter + sub * SUBLANES, SUBLANES)], cl.at[half * subs + sub])
+
+    class Spread:
+        def __init__(self, at, source, target):
+            self.at, self.source, self.target = at, source, target
+
+        def own(self):
+            return local(self.source, self.target(tm), al.at[self.at])
+
+        def pair(self):
+            return remote(self.source, self.target(tm), aps.at[self.at], apr.at[self.at], partner)
+
+        def across(self, o):
+            peer = lax.rem(tm_x + o, n_x)
+            return remote(
+                self.source, self.target(tm), axs.at[self.at, o], axr.at[self.at, o], {"tm": peer * 2 + core})
+
+        def relay(self, o):
+            held = self.target(lax.rem(tm_x + n_x - o, n_x) * 2 + core)
+            return remote(held, held, aqs.at[self.at, o], aqr.at[self.at, o], partner)
+
+        def begin(self):
+            for o in range(1, n_x):
+                self.across(o).start()
+            self.pair().start()
+            self.own().start()
+
+        def pass_on(self):
+            for o in range(1, n_x):
+                self.across(o).wait_recv()
+                self.relay(o).start()
+
+        def arrive(self):
+            self.own().wait()
+            self.pair().wait_recv()
+            for o in range(1, n_x):
+                self.relay(o).wait_recv()
+                self.relay(o).wait_send()
+
+        def end(self):
+            self.pair().wait_send()
+            for o in range(1, n_x):
+                self.across(o).wait_send()
+
+    guesses = Spread(0, guess, lambda t: guess_all.at[t])
+    firsts = Spread(1, tot.at[0], lambda t: own_first.at[pl.ds(t * quarter, quarter)])
+
+    def spread_rows(target, half, s, k, parts):
+        for j, value in enumerate(block_transpose(parts, lane, width)):
+            at = ((j * rows + half * SUBLANES) * SPIN + s) * local_k + k
+            target[pl.ds(at, SUBLANES, stride=SPIN * local_k), :] = value
+
+    def gather_rows(source, half, s, k):
+        parts = []
+        for t in range(n):
+            at = ((t * rows + half * SUBLANES) * SPIN + s) * local_k + k
+            parts.append(source[pl.ds(at, SUBLANES, stride=SPIN * local_k), :])
+        return jnp.concatenate(block_transpose(parts, lane, width), axis=0)
+
+    def first_layout(half):
+        @pl.loop(0, local_k, unroll=4)
+        def _(k):
+            for s in range(SPIN):
+                parts = [start[k, s, half * half_rows + g * SUBLANES:half * half_rows + (g + 1) * SUBLANES, :]
+                         for g in range(n)]
+                spread_rows(flat_snd, half, s, k, parts)
+
+    def keep_stack(n_pass, k, s, half, value):
+        for base, piece in ((0, value), (PANEL, rot(value))):
+            high, rest = split(piece)
+            at = pl.ds(pl.multiple_of(base + half * half_rows, half_rows), half_rows)
+            stk[n_pass, k, s, 0, at, :] = high
+            stk[n_pass, k, s, 1, at, :] = rest
+
+    def first_stack(half):
+        @pl.loop(0, half_chunks)
+        def _(d):
+            q = half * half_chunks + d
+            for o in range(1, n):
+                panel_out(q, o).wait_recv()
+            panel_own(q).wait()
+
+        @pl.loop(0, local_k, unroll=4)
+        def _(k):
+            for s in range(SPIN):
+                keep_stack(0, k, s, half, gather_rows(flat_rx_g, half, s, k))
+
+    def sigma(q):
+        @pl.loop(0, CHUNK)
+        def _(d):
+            i = q * CHUNK + d
+            both = jnp.concatenate(
+                [flat_recv[pl.ds(pl.multiple_of((i * SPIN + s) * K, K), K), :] for s in range(SPIN)], axis=1)
+            sums = dot3((fwd_split[0], fwd_split[1]), split(both))
+            site, mirrored = [], []
+            for s in range(SPIN):
+                with_cos = sums[:K, s * LANES:(s + 1) * LANES]
+                turned = rot(sums[K:, s * LANES:(s + 1) * LANES])
+                site.append(with_cos + turned)
+                mirrored.append(with_cos - turned)
+            first, second = site
+            flipped = swap(second)
+            pair = (first * jnp.where(low, second, flipped)
+                    + rot(first) * jnp.where(low, flipped, second)) * wvec[...]
+            pair_rot = rot(pair)
+            tops, bottoms = [], []
+            for s in range(SPIN):
+                other = mirrored[1 - s]
+                flipped = swap(other)
+                value = pair * jnp.where(low, other, flipped) - pair_rot * jnp.where(low, flipped, other)
+                tops.append(value)
+                bottoms.append(-rot(value))
+            stacked = jnp.concatenate(
+                [jnp.concatenate(tops, axis=1), jnp.concatenate(bottoms, axis=1)], axis=0)
+            result = dot3((back_split[0], back_split[1]), split(stacked))
+            for s in range(SPIN):
+                flat_sig[pl.ds(pl.multiple_of((i * SPIN + s) * K, K), K), :] = result[:, s * LANES:(s + 1) * LANES]
+
+    def send_sigma(n_pass, q):
+        for o in range(1, n):
+            sigma_out(n_pass, q, o).start()
+        sigma_own(n_pass, q).start()
+
+    def wait_sigma(n_pass, half):
+        @pl.loop(0, half_chunks)
+        def _(d):
+            q = half * half_chunks + d
+            for o in range(1, n):
+                sigma_out(n_pass, q, o).wait_recv()
+            sigma_own(n_pass, q).wait()
+
+    def second_sigma(q):
+        half = q // half_chunks
+
+        @pl.when(q % half_chunks == 0)
+        def _():
+            @pl.loop(0, per_half)
+            def _(d):
+                p = half * per_half + d
+                for o in range(1, n):
+                    next_out(p, o).wait_recv()
+                next_own(p).wait()
+
+        for o in range(1, n):
+            sigma_out(0, q, o).wait_send()
+        sigma(q)
+        send_sigma(1, q)
+
+    def convolve(n_pass, p):
+        half, sub, block = place(p)
+
+        @pl.when(p % per_half == 0)
+        def _():
+            wait_sigma(n_pass, half)
+
+        at = pl.ds(pl.multiple_of(half * half_rows, half_rows), half_rows)
+
+        @pl.loop(0, SUBLANES, unroll=SUBLANES)
+        def _(m):
+            k = block * quarter + sub * SUBLANES + m
+            for s in range(SPIN):
+                value = split(gather_rows(flat_rx_s, half, s, k))
+                out[k, s, at, :] = dot3(value, (stk[n_pass, k, s, 0], stk[n_pass, k, s, 1]), True)
+
+    def each(p, body):
+        half, sub, block = place(p)
+        at = pl.ds(pl.multiple_of(half * half_rows, half_rows), half_rows)
+
+        @pl.loop(0, SUBLANES)
+        def _(m):
+            k = block * quarter + sub * SUBLANES + m
+            for s in range(SPIN):
+                body(k, s, at, sub * SUBLANES + m)
+
+    def flows(n_pass, p):
+        block = place(p)[2]
+        if n_pass == 0:
+            yes = block >= 0
+            return yes, yes, yes, yes, yes
+        return block >= mom, block > mom, block <= mom, block < mom, block == mom
+
+    def origin(n_pass, p):
+        _, send_right, _, send_left, _ = flows(n_pass, p)
+
+        @pl.when(mom == 0)
+        def _():
+            def body(k, s, at, m):
+                rbuf[k, s, at, :] = out[k, s, at, :]
+            each(p, body)
+
+            @pl.when(send_right)
+            def _():
+                right_out(n_pass, p).start()
+
+        @pl.when(mom == n - 1)
+        def _():
+            def body(k, s, at, m):
+                lbuf[k, s, at, :] = out[k, s, at, :]
+            each(p, body)
+
+            @pl.when(send_left)
+            def _():
+                left_out(n_pass, p).start()
+
+    def near_step(n_pass, p):
+        from_left, send_right, from_right, send_left, _ = flows(n_pass, p)
+
+        @pl.when(near_left & (mom > 0) & from_left)
+        def _():
+            right_out(n_pass, p).wait_recv()
+
+            def body(k, s, at, m):
+                rbuf[k, s, at, :] = rbuf[k, s, at, :] + out[k, s, at, :]
+            each(p, body)
+
+            @pl.when(send_right)
+            def _():
+                right_out(n_pass, p).start()
+
+        @pl.when((mom >= n // 2) & (mom < n - 1) & from_right)
+        def _():
+            left_out(n_pass, p).wait_recv()
+
+            def body(k, s, at, m):
+                lbuf[k, s, at, :] = lbuf[k, s, at, :] + out[k, s, at, :]
+            each(p, body)
+
+            @pl.when(send_left)
+            def _():
+                left_out(n_pass, p).start()
+
+    def far_step(n_pass, p):
+        from_left, send_right, from_right, send_left, keep = flows(n_pass, p)
+
+        def one(mine, other, outer, send, copy):
+            copy.wait_recv()
+            if n_pass == 0:
+                def body(k, s, at, m):
+                    arrived, held = other[k, s, at, :], out[k, s, at, :]
+                    other[k, s, at, :] = arrived + held
+                    out[k, s, at, :] = mine[k, s, at, :] + arrived
+                each(p, body)
+            else:
+                @pl.when(send)
+                def _():
+                    def body(k, s, at, m):
+                        other[k, s, at, :] = other[k, s, at, :] + out[k, s, at, :]
+                    each(p, body)
+
+                @pl.when(keep)
+                def _():
+                    def body(k, s, at, m):
+                        tot[1, m, s, at, :] = mine[k, s, at, :] + other[k, s, at, :]
+                    each(p, body)
+
+            @pl.when(outer & send)
+            def _():
+                copy.start()
+
+        @pl.when(near_left & from_right)
+        def _():
+            one(rbuf, lbuf, mom > 0, send_left, left_out(n_pass, p))
+
+        @pl.when((mom >= n // 2) & from_left)
+        def _():
+            one(lbuf, rbuf, mom < n - 1, send_right, right_out(n_pass, p))
+
+    def update(p):
+        half, sub, block = place(p)
+        at = pl.ds(pl.multiple_of(half * half_rows, half_rows), half_rows)
+
+        @pl.when(block == mom)
+        def _():
+            def body(k, s, at, m):
+                tot[0, m, s, at, :] = out[k, s, at, :]
+            each(p, body)
+
+        @pl.loop(0, SUBLANES, unroll=SUBLANES)
+        def _(m):
+            k = block * quarter + sub * SUBLANES + m
+            for s in range(SPIN):
+                old = stk[0, k, s, 0, at, :].astype(jnp.float32) + stk[0, k, s, 1, at, :].astype(jnp.float32)
+                new = old + step_scale * dot3(split(out[k, s, at, :]), (stk[0, k, s, 0], stk[0, k, s, 1]))
+                keep_stack(1, k, s, half, new)
+                spread_rows(
+                    flat_snd, half, s, k, [new[g * SUBLANES:(g + 1) * SUBLANES, :] for g in range(n)])
+
+        for o in range(1, n):
+            next_out(p, o).start()
+        next_own(p).start()
+
+    def own_panel(group):
+        @pl.loop(0, SUBLANES, unroll=4)
+        def _(m):
+            k = group * SUBLANES + m
+            for s in range(SPIN):
+                first = start[k, s]
+                right = jnp.concatenate([first, rot(first)], axis=0)
+                own_first[k, s] = first + step_scale * dot3(split(own_first[k, s]), split(right))
+
+    def finish(sub):
+        is_block = chosen[...] > 0.5
+        for half in range(halves):
+            for o in range(1, n):
+                last_out(half, sub, o).wait_recv()
+            last_own(half, sub).wait()
+
+        @pl.loop(0, n * SUBLANES, unroll=4)
+        def _(d):
+            k = (d // SUBLANES) * quarter + sub * SUBLANES + d % SUBLANES
+            for s in range(SPIN):
+                whole = jnp.concatenate([own_last[half, k, s] for half in range(halves)], axis=0)
+                d_rows = jnp.concatenate([guess_all[t, k, s] for t in range(n)], axis=0)
+                right = jnp.where(is_block, whole, own_first[k, s])
+                left = jnp.where(is_block, d_rows, whole)
+                right = jnp.concatenate([right, rot(right)], axis=0)
+                out[k, s] = jnp.where(is_block, d_rows, start[k, s]) + step_scale * dot3(split(left), split(right))
+
+    first_layout(0)
+    pl.semaphore_wait(barrier, 2 * n - 2)
+    for half in range(halves):
+        if half > 0:
+            first_layout(half)
+        for q in range(half * half_chunks, (half + 1) * half_chunks):
+            for o in range(1, n):
+                forward(q, o).start()
+            forward_own(q).start()
+        if half == 0:
+            guesses.begin()
+
+    for at, table in enumerate(tables(ordering[...])):
+        fwd_split[0, at * K:(at + 1) * K, :], fwd_split[1, at * K:(at + 1) * K, :] = split(table)
+        turned = split(table.T)
+        back_split[0, :, at * K:(at + 1) * K], back_split[1, :, at * K:(at + 1) * K] = turned
+
+    @pl.loop(0, chunks + 1)
+    def _(q):
+        @pl.when(q < chunks)
+        def _():
+            for o in range(1, n):
+                forward(q, o).wait_recv()
+            forward_own(q).wait()
+            for o in range(1, n):
+                panel_out(q, o).start()
+            panel_own(q).start()
+            sigma(q)
+            send_sigma(0, q)
+
+        for half in range(halves - 1):
+            @pl.when(q == (half + 1) * half_chunks + 1)
+            def _():
+                first_stack(half)
+
+        @pl.when(q == chunks)
+        def _():
+            first_stack(halves - 1)
+
+    guesses.pass_on()
+
+    @pl.loop(0, chunks)
+    def _(q):
+        for o in range(1, n):
+            forward(q, o).wait_send()
+            panel_out(q, o).wait_send()
+
+    for o in range(1, n):
+        pl.semaphore_signal(room, inc=1, device_id={"tm": lax.rem(tm + o, n)}, device_id_type=MESH)
+
+    sigma_at = per_half + LAG + per_half + 1
+
+    @pl.loop(0, pieces + per_half + LAG)
+    def _(t):
+        @pl.when(t < pieces)
+        def _():
+            convolve(0, t)
+            origin(0, t)
+
+        @pl.when((t >= per_half) & (t - per_half < pieces))
+        def _():
+            near_step(0, t - per_half)
+
+        @pl.when(t >= per_half + LAG)
+        def _():
+            p = t - per_half - LAG
+            far_step(0, p)
+
+            @pl.when(p == 0)
+            def _():
+                pl.semaphore_wait(room, n - 1)
+
+            update(p)
+
+        @pl.when((t >= sigma_at) & (t < sigma_at + (halves - 1) * half_chunks))
+        def _():
+            second_sigma(t - sigma_at)
+
+    @pl.loop(0, pieces)
+    def _(p):
+        @pl.when(mom < n - 1)
+        def _():
+            right_out(0, p).wait_send()
+
+        @pl.when(mom > 0)
+        def _():
+            left_out(0, p).wait_send()
+
+    @pl.when(mom > 0)
+    def _():
+        pl.semaphore_signal(credit.at[1], inc=1, device_id={"mom": jnp.maximum(mom - 1, 0)}, device_id_type=MESH)
+
+    @pl.when(mom < n - 1)
+    def _():
+        pl.semaphore_signal(credit.at[0], inc=1, device_id={"mom": jnp.minimum(mom + 1, n - 1)}, device_id_type=MESH)
+
+    firsts.begin()
+
+    @pl.when(mom > 0)
+    def _():
+        pl.semaphore_wait(credit.at[0], 1)
+
+    @pl.when(mom < n - 1)
+    def _():
+        pl.semaphore_wait(credit.at[1], 1)
+
+    @pl.loop(0, pieces + LEAD + LAG)
+    def _(t):
+        @pl.when(t < pieces)
+        def _():
+            convolve(1, t)
+            origin(1, t)
+
+        @pl.when(t < half_chunks)
+        def _():
+            second_sigma((halves - 1) * half_chunks + t)
+
+        @pl.when((t >= LEAD) & (t - LEAD < pieces))
+        def _():
+            near_step(1, t - LEAD)
+
+        @pl.when(t >= LEAD + LAG)
+        def _():
+            p = t - LEAD - LAG
+            far_step(1, p)
+            half, sub, block = place(p)
+
+            @pl.when(block == mom)
+            def _():
+                for o in range(1, n):
+                    last_out(half, sub, o).start()
+                last_own(half, sub).start()
+
+        @pl.when(t == per_half)
+        def _():
+            firsts.pass_on()
+            firsts.arrive()
+
+        @pl.when((t >= per_half) & (t < per_half + local_k // SUBLANES))
+        def _():
+            own_panel(t - per_half)
+
+    guesses.arrive()
+    for sub in range(subs):
+        finish(sub)
+
+    @pl.loop(0, pieces)
+    def _(p):
+        _, send_right, _, send_left, _ = flows(1, p)
+
+        @pl.when((mom < n - 1) & send_right)
+        def _():
+            right_out(1, p).wait_send()
+
+        @pl.when((mom > 0) & send_left)
+        def _():
+            left_out(1, p).wait_send()
+
+        for o in range(1, n):
+            next_out(p, o).wait_send()
+
+    @pl.loop(0, chunks)
+    def _(q):
+        for o in range(1, n):
+            sigma_out(1, q, o).wait_send()
+
+    for half in range(halves):
+        for sub in range(subs):
+            for o in range(1, n):
+                last_out(half, sub, o).wait_send()
+    guesses.end()
+    firsts.end()
+
+
+def share_step(n, start, guess, ordering, wvec, chosen):
+    local_k = start.shape[0]
+    quarter, rows = local_k // n, PANEL // n
+    pieces = (rows // SUBLANES) * n * (quarter // SUBLANES)
+    chunks, ends = rows // CHUNK, (rows // SUBLANES) * (quarter // SUBLANES)
+    f32, bf16 = jnp.float32, jnp.bfloat16
+    dma = pltpu.SemaphoreType.DMA
+    vmem = pl.BlockSpec(memory_space=pltpu.VMEM)
+    moved = pltpu.VMEM((n, rows, SPIN, n, quarter, LANES), f32)
+    grid = pltpu.VMEM((rows, SPIN, n, n, quarter, LANES), f32)
+    square = (local_k, SPIN, PANEL, LANES)
+    return pl.pallas_call(
+        functools.partial(share_kernel, n),
+        out_shape=jax.ShapeDtypeStruct(start.shape, f32),
+        in_specs=[vmem] * 5,
+        out_specs=vmem,
+        scratch_shapes=[
+            moved, grid, grid, moved, moved,
+            pltpu.VMEM((PASSES, local_k, SPIN, 2, 2 * PANEL, LANES), bf16),
+            pltpu.VMEM(square, f32), pltpu.VMEM(square, f32),
+            pltpu.VMEM((PASSES, quarter, SPIN, PANEL, LANES), f32),
+            pltpu.VMEM((n,) + guess.shape, f32),
+            pltpu.VMEM((2, 2 * K, K), bf16),
+            pltpu.VMEM((2, K, 2 * K), bf16),
+            dma((chunks,)), dma((chunks, n)), dma((chunks, n)),
+            dma((chunks,)), dma((chunks, n)), dma((chunks, n)),
+            dma((PASSES, chunks)), dma((PASSES, chunks, n)), dma((PASSES, chunks, n)),
+            dma((pieces,)), dma((pieces, n)), dma((pieces, n)),
+            dma((PASSES, pieces)), dma((PASSES, pieces)), dma((PASSES, pieces)), dma((PASSES, pieces)),
+            pltpu.SemaphoreType.REGULAR((2,)), pltpu.SemaphoreType.REGULAR,
+            dma((ends,)), dma((ends, n)), dma((ends, n)),
+            dma((2,)), dma((2,)), dma((2,)), dma((2, n)), dma((2, n)), dma((2, n)), dma((2, n)),
+        ],
+        compiler_params=pltpu.CompilerParams(
+            collective_id=0, has_side_effects=True, vmem_limit_bytes=63 * 1024 * 1024),
+        name="share_step",
+    )(start, guess, ordering, wvec, chosen)
+
+
 def body(panel_start, block_guess, coupling, slab_owner, expiring, ordering):
     slab_count = lax.axis_size("tm")
     n_mom = lax.axis_size("mom")
@@ -381,13 +1057,20 @@
     slab_mine = jnp.sum(blocks * (slab_owner == own_index).astype(jnp.int32))
     position = (slab_mine - expiring[0]) % slab_count
     window = slab_count * PANEL
-    times = position * PANEL + jnp.arange(PANEL, dtype=jnp.int32)
+    local_k = panel_start.shape[0]
+    shared = n_mom == slab_count and local_k % (SUBLANES * slab_count) == 0 and PANEL % (SUBLANES * slab_count) == 0
+    within = jnp.arange(PANEL, dtype=jnp.int32)
+    if shared:
+        share = PANEL // n_mom
+        within = lax.axis_index("mom") * share + within % share
+    times = position * PANEL + within
     weights = jnp.exp(-1.5 * (window - 1 - times).astype(jnp.float32) / window) / math.sqrt(window)
     strength = coupling[0] * coupling[0]
     wvec = (strength * jnp.concatenate([weights, weights]))[None, :]
     owner_expiring = jnp.sum(slab_owner * (blocks == expiring[0]).astype(jnp.int32))
     chosen = jnp.broadcast_to((own_index == owner_expiring).astype(jnp.float32), (1, LANES))
-    local_k = panel_start.shape[0]
+    if shared:
+        return share_step(n_mom, panel_start, block_guess, ordering[None, :], wvec, chosen)
     start = panel_start.reshape(local_k, SPIN, CHUNKS, PANEL // CHUNKS, LANES)
     result = panel_step(n_mom, slab_count, start, block_guess, ordering[None, :], wvec, chosen)
     return result.reshape(panel_start.shape)

time: 427 us -> 388 us (0.909)
  the two profiles are of different devices: /device:TPU:28 before, /device:TPU:0 now
where the time goes in v1:
time: 388 us; the launch traced here: 382 us
  Pallas kernels  372 us (96%)
  local copies, waits for them, and re-layouts  5.31 us (1%)
    pallas_call x1, Pallas kernels, share_step(): pl.pallas_call(functools.partial(share_kernel, n), out_shape=jax.ShapeDty...  372 us

profile of v1, /device:TPU:0, one launch (start us, length us, event | category | flops | bytes accessed | tf_op | source)
XLA Modules:
  0.0 381.7 jit_solution(5825309873262343208)
XLA Ops:
  1.3 1.3 fusion.9
  3.9 0.6 maximum_multiply_fusion.wvec
  4.4 0.5 broadcast_in_dim.8.chosen
  5.0 371.9 %share_step.1 = f32[64,2,64,128]{3,2,1,0:T(8,128)} custom-call(f32[64,2,64,128]{3,2,1,0:T(8,128)} %start.1, f32[64,2,16,128]{3,2,1,0:T(8,128)} %guess.1, s32[1,256]{1,0:T(1,128)} %bitcast.7, f32[1,128]{1,0:T(1,128)} %maximum_multiply_fusion.wvec, f32[1,128]{1,0:T(1,128)} %broadcast_in_dim.8.chosen), custom_call_target="tpu_custom_call" | custom-call | tf_op jit(solution)/shard_map/share_step/pallas_call | solution.py:1024
  376.9 4.8 %copy.10 = f32[64,2,64,128]{3,2,1,0:T(8,128)} copy(f32[64,2,64,128]{3,2,1,0:T(8,128)} %share_step.1) | data formatting | bytes 8388608
  (1 shorter events, 0.0 us)

commit v2 on v1

--- a/solution.py
+++ b/solution.py
@@ -375,8 +375,9 @@
 
 SUBLANES = 8
 CHUNK = 2
-LAG = 2
-LEAD = 2
+AHEAD = 3
+LAG = 3
+LEAD = (8, 4)
 
 
 def block_transpose(blocks, lane, width):
@@ -394,9 +395,9 @@
 
 
 def share_kernel(
-    n, start, guess, ordering, wvec, chosen,
-    out, snd, recv, sig, rx_g, rx_s, stk, rbuf, lbuf, tot, guess_all, fwd_split, back_split,
-    fl, fs, fr, gl, gs, gr, sl, ss, sr, tl, ts, tr, rs, rr, ls, lr, credit, room, cl, cs, cr,
+    n, start, guess, ordering, coupling, slab_owner, expiring,
+    out, snd, recv, sig, rx_g, rx_s, stk_a, stk_b, wvec, rbuf, lbuf, tot, guess_all, fwd_split, back_split,
+    fl, fs, fr, gl, gs, gr, sl, ss, sr, tl, ts, tr, rs, rr, ls, lr, credit, room,
     al, aps, apr, axs, axr, aqs, aqr,
 ):
     mom, tm = lax.axis_index("mom"), lax.axis_index("tm")
@@ -407,7 +408,7 @@
     halves = rows // SUBLANES
     half_rows = n * SUBLANES
     subs = quarter // SUBLANES
-    per_half = n * subs
+    per_half = n * subs * SPIN
     pieces = halves * per_half
     chunks = rows // CHUNK
     half_chunks = SUBLANES // CHUNK
@@ -420,11 +421,11 @@
     sign = jnp.where(low, -1.0, 1.0).astype(jnp.float32)
     flat = n * rows * SPIN * local_k
     flat_snd = snd.reshape(flat, LANES)
-    flat_recv = recv.reshape(flat, LANES)
-    flat_sig = sig.reshape(flat, LANES)
     flat_rx_g = rx_g.reshape(flat, LANES)
     flat_rx_s = rx_s.reshape(flat, LANES)
-    own_first = rx_g.reshape(local_k, SPIN, PANEL, LANES)
+    own_first = rx_g.reshape(local_k, SPIN, halves, half_rows, LANES)
+    part = out.reshape(local_k, SPIN, halves, half_rows, LANES)
+    stacks = (stk_a, stk_b)
     own_last = recv.reshape(halves, local_k, SPIN, half_rows, LANES)
     near_left = mom < n // 2
 
@@ -475,50 +476,38 @@
 
     def place(p):
         half, rest = p // per_half, p % per_half
-        sub, turn = rest // n, rest % n
+        group, turn = rest // n, rest % n
         odd = turn % 2
         block = (1 - odd) * (n - 1 - turn // 2) + odd * (turn // 2)
-        return half, sub, block
+        return half, group // SPIN, group % SPIN, block
 
     def next_out(p, o):
-        half, sub, block = place(p)
+        half, sub, s, block = place(p)
         peer = lax.rem(tm + o, n)
         at, ks = pl.ds(half * SUBLANES, SUBLANES), pl.ds(sub * SUBLANES, SUBLANES)
         return remote(
-            snd.at[peer, at, :, block, ks], recv.at[at, :, block, tm, ks], ts.at[p, o], tr.at[p, o], {"tm": peer})
+            snd.at[peer, at, s, block, ks], recv.at[at, s, block, tm, ks], ts.at[p, o], tr.at[p, o], {"tm": peer})
 
     def next_own(p):
-        half, sub, block = place(p)
+        half, sub, s, block = place(p)
         at, ks = pl.ds(half * SUBLANES, SUBLANES), pl.ds(sub * SUBLANES, SUBLANES)
-        return local(snd.at[tm, at, :, block, ks], recv.at[at, :, block, tm, ks], tl.at[p])
+        return local(snd.at[tm, at, s, block, ks], recv.at[at, s, block, tm, ks], tl.at[p])
 
     def window(p):
-        half, sub, block = place(p)
-        return pl.ds(block * quarter + sub * SUBLANES, SUBLANES), pl.ds(half * half_rows, half_rows)
+        half, sub, s, block = place(p)
+        return pl.ds(block * quarter + sub * SUBLANES, SUBLANES), s, half
 
     def right_out(n_pass, p):
-        ks, at = window(p)
+        at = window(p)
         return remote(
-            rbuf.at[ks, :, at], rbuf.at[ks, :, at], rs.at[n_pass, p], rr.at[n_pass, p],
+            rbuf.at[at], rbuf.at[at], rs.at[n_pass, p], rr.at[n_pass, p],
             {"mom": jnp.minimum(mom + 1, n - 1)})
 
     def left_out(n_pass, p):
-        ks, at = window(p)
+        at = window(p)
         return remote(
-            lbuf.at[ks, :, at], lbuf.at[ks, :, at], ls.at[n_pass, p], lr.at[n_pass, p],
+            lbuf.at[at], lbuf.at[at], ls.at[n_pass, p], lr.at[n_pass, p],
             {"mom": jnp.maximum(mom - 1, 0)})
-
-    def last_out(half, sub, o):
-        at = half * subs + sub
-        return remote(
-            tot.at[1, pl.ds(sub * SUBLANES, SUBLANES), :, pl.ds(half * half_rows, half_rows)],
-            own_last.at[half, pl.ds(tm * quarter + sub * SUBLANES, SUBLANES)],
-            cs.at[at, o], cr.at[at, o], {"tm": lax.rem(tm + o, n)})
-
-    def last_own(half, sub):
-        return local(
-            tot.at[1, pl.ds(sub * SUBLANES, SUBLANES), :, pl.ds(half * half_rows, half_rows)],
-            own_last.at[half, pl.ds(tm * quarter + sub * SUBLANES, SUBLANES)], cl.at[half * subs + sub])
 
     class Spread:
         def __init__(self, at, source, target):
@@ -563,7 +552,14 @@
                 self.across(o).wait_send()
 
     guesses = Spread(0, guess, lambda t: guess_all.at[t])
-    firsts = Spread(1, tot.at[0], lambda t: own_first.at[pl.ds(t * quarter, quarter)])
+    firsts = [
+        Spread(1 + half, tot.at[0, :, :, half], lambda t, half=half: own_first.at[pl.ds(t * quarter, quarter), :, half])
+        for half in range(halves)]
+
+    def lasts(half, sub, s):
+        return Spread(
+            1 + halves + (half * subs + sub) * SPIN + s, tot.at[1, pl.ds(sub * SUBLANES, SUBLANES), s, half],
+            lambda t: own_last.at[half, pl.ds(t * quarter + sub * SUBLANES, SUBLANES), s])
 
     def spread_rows(target, half, s, k, parts):
         for j, value in enumerate(block_transpose(parts, lane, width)):
@@ -586,11 +582,11 @@
                 spread_rows(flat_snd, half, s, k, parts)
 
     def keep_stack(n_pass, k, s, half, value):
-        for base, piece in ((0, value), (PANEL, rot(value))):
-            high, rest = split(piece)
-            at = pl.ds(pl.multiple_of(base + half * half_rows, half_rows), half_rows)
-            stk[n_pass, k, s, 0, at, :] = high
-            stk[n_pass, k, s, 1, at, :] = rest
+        for at, piece in enumerate((value, rot(value))):
+            stacks[n_pass][k, s, 0, at, half], stacks[n_pass][k, s, 1, at, half] = split(piece)
+
+    def stack_of(n_pass, k, s):
+        return tuple(stacks[n_pass][k, s, at].reshape(2 * PANEL, LANES) for at in range(2))
 
     def first_stack(half):
         @pl.loop(0, half_chunks)
@@ -610,7 +606,7 @@
         def _(d):
             i = q * CHUNK + d
             both = jnp.concatenate(
-                [flat_recv[pl.ds(pl.multiple_of((i * SPIN + s) * K, K), K), :] for s in range(SPIN)], axis=1)
+                [recv[i, s].reshape(K, LANES) for s in range(SPIN)], axis=1)
             sums = dot3((fwd_split[0], fwd_split[1]), split(both))
             site, mirrored = [], []
             for s in range(SPIN):
@@ -634,7 +630,7 @@
                 [jnp.concatenate(tops, axis=1), jnp.concatenate(bottoms, axis=1)], axis=0)
             result = dot3((back_split[0], back_split[1]), split(stacked))
             for s in range(SPIN):
-                flat_sig[pl.ds(pl.multiple_of((i * SPIN + s) * K, K), K), :] = result[:, s * LANES:(s + 1) * LANES]
+                sig[i, s] = result[:, s * LANES:(s + 1) * LANES].reshape(sig.shape[2:])
 
     def send_sigma(n_pass, q):
         for o in range(1, n):
@@ -667,33 +663,29 @@
         send_sigma(1, q)
 
     def convolve(n_pass, p):
-        half, sub, block = place(p)
+        half, sub, s, block = place(p)
 
         @pl.when(p % per_half == 0)
         def _():
             wait_sigma(n_pass, half)
 
-        at = pl.ds(pl.multiple_of(half * half_rows, half_rows), half_rows)
-
-        @pl.loop(0, SUBLANES, unroll=SUBLANES)
-        def _(m):
+        results = []
+        for m in range(SUBLANES):
             k = block * quarter + sub * SUBLANES + m
-            for s in range(SPIN):
-                value = split(gather_rows(flat_rx_s, half, s, k))
-                out[k, s, at, :] = dot3(value, (stk[n_pass, k, s, 0], stk[n_pass, k, s, 1]), True)
+            value = split(gather_rows(flat_rx_s, half, s, k))
+            results.append((k, dot3(value, stack_of(n_pass, k, s), True)))
+        for k, result in results:
+            part[k, s, half] = result
 
     def each(p, body):
-        half, sub, block = place(p)
-        at = pl.ds(pl.multiple_of(half * half_rows, half_rows), half_rows)
-
-        @pl.loop(0, SUBLANES)
-        def _(m):
-            k = block * quarter + sub * SUBLANES + m
-            for s in range(SPIN):
-                body(k, s, at, sub * SUBLANES + m)
+        half, sub, s, block = place(p)
+        done = [body((block * quarter + sub * SUBLANES + m, s, half), sub * SUBLANES + m) for m in range(SUBLANES)]
+        for stores in done:
+            for target, at, value in stores:
+                target[at] = value
 
     def flows(n_pass, p):
-        block = place(p)[2]
+        block = place(p)[3]
         if n_pass == 0:
             yes = block >= 0
             return yes, yes, yes, yes, yes
@@ -704,9 +696,7 @@
 
         @pl.when(mom == 0)
         def _():
-            def body(k, s, at, m):
-                rbuf[k, s, at, :] = out[k, s, at, :]
-            each(p, body)
+            each(p, lambda at, m: [(rbuf, at, part[at])])
 
             @pl.when(send_right)
             def _():
@@ -714,9 +704,7 @@
 
         @pl.when(mom == n - 1)
         def _():
-            def body(k, s, at, m):
-                lbuf[k, s, at, :] = out[k, s, at, :]
-            each(p, body)
+            each(p, lambda at, m: [(lbuf, at, part[at])])
 
             @pl.when(send_left)
             def _():
@@ -729,9 +717,7 @@
         def _():
             right_out(n_pass, p).wait_recv()
 
-            def body(k, s, at, m):
-                rbuf[k, s, at, :] = rbuf[k, s, at, :] + out[k, s, at, :]
-            each(p, body)
+            each(p, lambda at, m: [(rbuf, at, rbuf[at] + part[at])])
 
             @pl.when(send_right)
             def _():
@@ -741,9 +727,7 @@
         def _():
             left_out(n_pass, p).wait_recv()
 
-            def body(k, s, at, m):
-                lbuf[k, s, at, :] = lbuf[k, s, at, :] + out[k, s, at, :]
-            each(p, body)
+            each(p, lambda at, m: [(lbuf, at, lbuf[at] + part[at])])
 
             @pl.when(send_left)
             def _():
@@ -755,23 +739,16 @@
         def one(mine, other, outer, send, copy):
             copy.wait_recv()
             if n_pass == 0:
-                def body(k, s, at, m):
-                    arrived, held = other[k, s, at, :], out[k, s, at, :]
-                    other[k, s, at, :] = arrived + held
-                    out[k, s, at, :] = mine[k, s, at, :] + arrived
-                each(p, body)
+                each(p, lambda at, m: [
+                    (other, at, other[at] + part[at]), (part, at, mine[at] + other[at])])
             else:
                 @pl.when(send)
                 def _():
-                    def body(k, s, at, m):
-                        other[k, s, at, :] = other[k, s, at, :] + out[k, s, at, :]
-                    each(p, body)
+                    each(p, lambda at, m: [(other, at, other[at] + part[at])])
 
                 @pl.when(keep)
                 def _():
-                    def body(k, s, at, m):
-                        tot[1, m, s, at, :] = mine[k, s, at, :] + other[k, s, at, :]
-                    each(p, body)
+                    each(p, lambda at, m: [(tot, (1, m) + at[1:], mine[at] + other[at])])
 
             @pl.when(outer & send)
             def _():
@@ -786,73 +763,88 @@
             one(lbuf, rbuf, mom < n - 1, send_right, right_out(n_pass, p))
 
     def update(p):
-        half, sub, block = place(p)
-        at = pl.ds(pl.multiple_of(half * half_rows, half_rows), half_rows)
+        half, sub, s, block = place(p)
 
         @pl.when(block == mom)
         def _():
-            def body(k, s, at, m):
-                tot[0, m, s, at, :] = out[k, s, at, :]
-            each(p, body)
-
-        @pl.loop(0, SUBLANES, unroll=SUBLANES)
-        def _(m):
+            each(p, lambda at, m: [(tot, (0, m) + at[1:], part[at])])
+
+        results = []
+        for m in range(SUBLANES):
             k = block * quarter + sub * SUBLANES + m
-            for s in range(SPIN):
-                old = stk[0, k, s, 0, at, :].astype(jnp.float32) + stk[0, k, s, 1, at, :].astype(jnp.float32)
-                new = old + step_scale * dot3(split(out[k, s, at, :]), (stk[0, k, s, 0], stk[0, k, s, 1]))
-                keep_stack(1, k, s, half, new)
-                spread_rows(
-                    flat_snd, half, s, k, [new[g * SUBLANES:(g + 1) * SUBLANES, :] for g in range(n)])
+            old = stk_a[k, s, 0, 0, half].astype(jnp.float32) + stk_a[k, s, 1, 0, half].astype(jnp.float32)
+            results.append((k, old + step_scale * dot3(split(part[k, s, half]), stack_of(0, k, s))))
+        for k, new in results:
+            keep_stack(1, k, s, half, new)
+            spread_rows(flat_snd, half, s, k, [new[g * SUBLANES:(g + 1) * SUBLANES, :] for g in range(n)])
 
         for o in range(1, n):
             next_out(p, o).start()
         next_own(p).start()
 
     def own_panel(group):
-        @pl.loop(0, SUBLANES, unroll=4)
-        def _(m):
-            k = group * SUBLANES + m
+        results = []
+        for m in range(SUBLANES // 2):
+            k = group * (SUBLANES // 2) + m
             for s in range(SPIN):
                 first = start[k, s]
-                right = jnp.concatenate([first, rot(first)], axis=0)
-                own_first[k, s] = first + step_scale * dot3(split(own_first[k, s]), split(right))
-
-    def finish(sub):
-        is_block = chosen[...] > 0.5
+                right = split(jnp.concatenate([first, rot(first)], axis=0))
+                new = first + step_scale * dot3(split(own_first[k, s].reshape(PANEL, LANES)), right)
+                results.append((k, s, new))
+        for k, s, new in results:
+            own_first[k, s] = new.reshape(halves, half_rows, LANES)
+
+    def finish(sub, s):
+        is_block = chosen > 0.5
         for half in range(halves):
-            for o in range(1, n):
-                last_out(half, sub, o).wait_recv()
-            last_own(half, sub).wait()
-
-        @pl.loop(0, n * SUBLANES, unroll=4)
-        def _(d):
-            k = (d // SUBLANES) * quarter + sub * SUBLANES + d % SUBLANES
-            for s in range(SPIN):
+            lasts(half, sub, s).arrive()
+
+        @pl.loop(0, n)
+        def _(t):
+            results = []
+            for m in range(SUBLANES):
+                k = t * quarter + sub * SUBLANES + m
                 whole = jnp.concatenate([own_last[half, k, s] for half in range(halves)], axis=0)
-                d_rows = jnp.concatenate([guess_all[t, k, s] for t in range(n)], axis=0)
-                right = jnp.where(is_block, whole, own_first[k, s])
+                d_rows = jnp.concatenate([guess_all[at, k, s] for at in range(n)], axis=0)
+                right = jnp.where(is_block, whole, own_first[k, s].reshape(PANEL, LANES))
                 left = jnp.where(is_block, d_rows, whole)
-                right = jnp.concatenate([right, rot(right)], axis=0)
-                out[k, s] = jnp.where(is_block, d_rows, start[k, s]) + step_scale * dot3(split(left), split(right))
+                right = split(jnp.concatenate([right, rot(right)], axis=0))
+                new = jnp.where(is_block, d_rows, start[k, s]) + step_scale * dot3(split(left), right)
+                results.append((k, new))
+            for k, new in results:
+                out[k, s] = new
+
+    def begin_forward(q):
+        for o in range(1, n):
+            forward(q, o).start()
+        forward_own(q).start()
 
     first_layout(0)
     pl.semaphore_wait(barrier, 2 * n - 2)
-    for half in range(halves):
-        if half > 0:
-            first_layout(half)
-        for q in range(half * half_chunks, (half + 1) * half_chunks):
-            for o in range(1, n):
-                forward(q, o).start()
-            forward_own(q).start()
-        if half == 0:
-            guesses.begin()
+    for q in range(min(AHEAD, half_chunks)):
+        begin_forward(q)
+    for half in range(1, halves):
+        first_layout(half)
 
     for at, table in enumerate(tables(ordering[...])):
         fwd_split[0, at * K:(at + 1) * K, :], fwd_split[1, at * K:(at + 1) * K, :] = split(table)
         turned = split(table.T)
         back_split[0, :, at * K:(at + 1) * K], back_split[1, :, at * K:(at + 1) * K] = turned
 
+    owners = slab_owner[...].astype(jnp.float32)
+    slabs = lax.broadcasted_iota(jnp.int32, owners.shape, 1).astype(jnp.float32)
+    oldest = expiring[...].astype(jnp.float32)
+    mine = tm.astype(jnp.float32)
+    slab_mine = jnp.sum(jnp.where(owners == mine, slabs, 0.0), axis=1, keepdims=True)
+    owner_expiring = jnp.sum(jnp.where(slabs == oldest, owners, 0.0), axis=1, keepdims=True)
+    position = slab_mine - oldest
+    position = jnp.where(position < 0.0, position + n, position)
+    within = (mom * rows + lane % rows).astype(jnp.float32)
+    ahead = (n * PANEL - 1) - (position * PANEL + within)
+    strength = coupling[...] * coupling[...]
+    wvec[...] = strength * (jnp.exp(-1.5 * ahead / (n * PANEL)) / math.sqrt(n * PANEL))
+    chosen = jnp.where(owner_expiring == mine, jnp.ones((1, LANES), jnp.float32), 0.0)
+
     @pl.loop(0, chunks + 1)
     def _(q):
         @pl.when(q < chunks)
@@ -860,6 +852,11 @@
             for o in range(1, n):
                 forward(q, o).wait_recv()
             forward_own(q).wait()
+
+            @pl.when(q + AHEAD < chunks)
+            def _():
+                begin_forward(q + AHEAD)
+
             for o in range(1, n):
                 panel_out(q, o).start()
             panel_own(q).start()
@@ -875,8 +872,6 @@
         def _():
             first_stack(halves - 1)
 
-    guesses.pass_on()
-
     @pl.loop(0, chunks)
     def _(q):
         for o in range(1, n):
@@ -885,23 +880,26 @@
 
     for o in range(1, n):
         pl.semaphore_signal(room, inc=1, device_id={"tm": lax.rem(tm + o, n)}, device_id_type=MESH)
-
-    sigma_at = per_half + LAG + per_half + 1
-
-    @pl.loop(0, pieces + per_half + LAG)
+    guesses.begin()
+
+    lead = LEAD[0]
+    told = per_half + lead + LAG
+    sigma_at = told + 3
+
+    @pl.loop(0, pieces + lead + LAG)
     def _(t):
         @pl.when(t < pieces)
         def _():
             convolve(0, t)
             origin(0, t)
 
-        @pl.when((t >= per_half) & (t - per_half < pieces))
-        def _():
-            near_step(0, t - per_half)
-
-        @pl.when(t >= per_half + LAG)
-        def _():
-            p = t - per_half - LAG
+        @pl.when((t >= lead) & (t - lead < pieces))
+        def _():
+            near_step(0, t - lead)
+
+        @pl.when(t >= lead + LAG)
+        def _():
+            p = t - lead - LAG
             far_step(0, p)
 
             @pl.when(p == 0)
@@ -910,9 +908,20 @@
 
             update(p)
 
-        @pl.when((t >= sigma_at) & (t < sigma_at + (halves - 1) * half_chunks))
-        def _():
-            second_sigma(t - sigma_at)
+        for half in range(halves - 1):
+            @pl.when(t == told + half * per_half)
+            def _():
+                firsts[half].begin()
+
+        @pl.when(t == told)
+        def _():
+            guesses.pass_on()
+
+        d = t - sigma_at
+
+        @pl.when((d >= 0) & (d < 2 * (halves - 1) * half_chunks) & (d % 2 == 0))
+        def _():
+            second_sigma(d // 2)
 
     @pl.loop(0, pieces)
     def _(p):
@@ -932,8 +941,6 @@
     def _():
         pl.semaphore_signal(credit.at[0], inc=1, device_id={"mom": jnp.minimum(mom + 1, n - 1)}, device_id_type=MESH)
 
-    firsts.begin()
-
     @pl.when(mom > 0)
     def _():
         pl.semaphore_wait(credit.at[0], 1)
@@ -942,45 +949,56 @@
     def _():
         pl.semaphore_wait(credit.at[1], 1)
 
-    @pl.loop(0, pieces + LEAD + LAG)
+    lead = LEAD[1]
+    panel_at = 2 * per_half - 2 * local_k // SUBLANES + 6
+
+    @pl.loop(0, pieces + lead + LAG)
     def _(t):
         @pl.when(t < pieces)
         def _():
             convolve(1, t)
             origin(1, t)
 
-        @pl.when(t < half_chunks)
-        def _():
-            second_sigma((halves - 1) * half_chunks + t)
-
-        @pl.when((t >= LEAD) & (t - LEAD < pieces))
-        def _():
-            near_step(1, t - LEAD)
-
-        @pl.when(t >= LEAD + LAG)
-        def _():
-            p = t - LEAD - LAG
+        @pl.when((t >= 4) & (t < 4 + 2 * half_chunks) & (t % 2 == 0))
+        def _():
+            second_sigma((halves - 1) * half_chunks + (t - 4) // 2)
+
+        @pl.when((t >= lead) & (t - lead < pieces))
+        def _():
+            near_step(1, t - lead)
+
+        @pl.when(t >= lead + LAG)
+        def _():
+            p = t - lead - LAG
             far_step(1, p)
-            half, sub, block = place(p)
+            half, sub, s, block = place(p)
 
             @pl.when(block == mom)
             def _():
-                for o in range(1, n):
-                    last_out(half, sub, o).start()
-                last_own(half, sub).start()
-
-        @pl.when(t == per_half)
-        def _():
-            firsts.pass_on()
-            firsts.arrive()
-
-        @pl.when((t >= per_half) & (t < per_half + local_k // SUBLANES))
-        def _():
-            own_panel(t - per_half)
+                lasts(half, sub, s).begin()
+
+        @pl.when(t == 4 + 2 * half_chunks)
+        def _():
+            firsts[halves - 1].begin()
+
+        @pl.when(t == panel_at)
+        def _():
+            for first in firsts:
+                first.pass_on()
+            for first in firsts:
+                first.arrive()
+
+        @pl.when((t >= panel_at) & (t < panel_at + 2 * local_k // SUBLANES))
+        def _():
+            own_panel(t - panel_at)
 
     guesses.arrive()
-    for sub in range(subs):
-        finish(sub)
+
+    @pl.loop(0, subs * SPIN)
+    def _(d):
+        for half in range(halves):
+            lasts(half, d // SPIN, d % SPIN).pass_on()
+        finish(d // SPIN, d % SPIN)
 
     @pl.loop(0, pieces)
     def _(p):
@@ -1003,34 +1021,38 @@
             sigma_out(1, q, o).wait_send()
 
     for half in range(halves):
-        for sub in range(subs):
-            for o in range(1, n):
-                last_out(half, sub, o).wait_send()
+        @pl.loop(0, subs * SPIN)
+        def _(d):
+            lasts(half, d // SPIN, d % SPIN).end()
     guesses.end()
-    firsts.end()
-
-
-def share_step(n, start, guess, ordering, wvec, chosen):
+    for first in firsts:
+        first.end()
+
+
+def share_step(n, start, guess, ordering, coupling, slab_owner, expiring):
     local_k = start.shape[0]
     quarter, rows = local_k // n, PANEL // n
-    pieces = (rows // SUBLANES) * n * (quarter // SUBLANES)
-    chunks, ends = rows // CHUNK, (rows // SUBLANES) * (quarter // SUBLANES)
+    halves, subs = rows // SUBLANES, quarter // SUBLANES
+    pieces, chunks = halves * n * subs * SPIN, rows // CHUNK
+    spreads = 1 + halves + halves * subs * SPIN
+    half_rows = n * SUBLANES
     f32, bf16 = jnp.float32, jnp.bfloat16
     dma = pltpu.SemaphoreType.DMA
     vmem = pl.BlockSpec(memory_space=pltpu.VMEM)
     moved = pltpu.VMEM((n, rows, SPIN, n, quarter, LANES), f32)
     grid = pltpu.VMEM((rows, SPIN, n, n, quarter, LANES), f32)
-    square = (local_k, SPIN, PANEL, LANES)
+    square = (local_k, SPIN, halves, half_rows, LANES)
+    stack = pltpu.VMEM((local_k, SPIN, 2, 2, halves, half_rows, LANES), bf16)
     return pl.pallas_call(
         functools.partial(share_kernel, n),
         out_shape=jax.ShapeDtypeStruct(start.shape, f32),
-        in_specs=[vmem] * 5,
+        in_specs=[vmem] * 6,
         out_specs=vmem,
         scratch_shapes=[
             moved, grid, grid, moved, moved,
-            pltpu.VMEM((PASSES, local_k, SPIN, 2, 2 * PANEL, LANES), bf16),
+            stack, stack, pltpu.VMEM((1, LANES), f32),
             pltpu.VMEM(square, f32), pltpu.VMEM(square, f32),
-            pltpu.VMEM((PASSES, quarter, SPIN, PANEL, LANES), f32),
+            pltpu.VMEM((PASSES, quarter) + square[1:], f32),
             pltpu.VMEM((n,) + guess.shape, f32),
             pltpu.VMEM((2, 2 * K, K), bf16),
             pltpu.VMEM((2, K, 2 * K), bf16),
@@ -1040,37 +1062,34 @@
             dma((pieces,)), dma((pieces, n)), dma((pieces, n)),
             dma((PASSES, pieces)), dma((PASSES, pieces)), dma((PASSES, pieces)), dma((PASSES, pieces)),
             pltpu.SemaphoreType.REGULAR((2,)), pltpu.SemaphoreType.REGULAR,
-            dma((ends,)), dma((ends, n)), dma((ends, n)),
-            dma((2,)), dma((2,)), dma((2,)), dma((2, n)), dma((2, n)), dma((2, n)), dma((2, n)),
+            dma((spreads,)), dma((spreads,)), dma((spreads,)),
+            dma((spreads, n)), dma((spreads, n)), dma((spreads, n)), dma((spreads, n)),
         ],
         compiler_params=pltpu.CompilerParams(
             collective_id=0, has_side_effects=True, vmem_limit_bytes=63 * 1024 * 1024),
         name="share_step",
-    )(start, guess, ordering, wvec, chosen)
+    )(start, guess, ordering, coupling, slab_owner, expiring)
 
 
 def body(panel_start, block_guess, coupling, slab_owner, expiring, ordering):
     slab_count = lax.axis_size("tm")
     n_mom = lax.axis_size("mom")
+    local_k = panel_start.shape[0]
+    unit = SUBLANES * slab_count
+    if n_mom == slab_count and local_k % unit == 0 and PANEL % unit == 0:
+        return share_step(
+            n_mom, panel_start, block_guess, ordering[None, :], coupling[None, :], slab_owner[None, :], expiring[None, :])
     own_index = lax.axis_index("tm")
     blocks = jnp.arange(slab_count, dtype=jnp.int32)
     slab_mine = jnp.sum(blocks * (slab_owner == own_index).astype(jnp.int32))
     position = (slab_mine - expiring[0]) % slab_count
     window = slab_count * PANEL
-    local_k = panel_start.shape[0]
-    shared = n_mom == slab_count and local_k % (SUBLANES * slab_count) == 0 and PANEL % (SUBLANES * slab_count) == 0
-    within = jnp.arange(PANEL, dtype=jnp.int32)
-    if shared:
-        share = PANEL // n_mom
-        within = lax.axis_index("mom") * share + within % share
-    times = position * PANEL + within
+    times = position * PANEL + jnp.arange(PANEL, dtype=jnp.int32)
     weights = jnp.exp(-1.5 * (window - 1 - times).astype(jnp.float32) / window) / math.sqrt(window)
     strength = coupling[0] * coupling[0]
     wvec = (strength * jnp.concatenate([weights, weights]))[None, :]
     owner_expiring = jnp.sum(slab_owner * (blocks == expiring[0]).astype(jnp.int32))
     chosen = jnp.broadcast_to((own_index == owner_expiring).astype(jnp.float32), (1, LANES))
-    if shared:
-        return share_step(n_mom, panel_start, block_guess, ordering[None, :], wvec, chosen)
     start = panel_start.reshape(local_k, SPIN, CHUNKS, PANEL // CHUNKS, LANES)
     result = panel_step(n_mom, slab_count, start, block_guess, ordering[None, :], wvec, chosen)
     return result.reshape(panel_start.shape)

time: 388 us -> 356 us (0.918); the launches traced: 382 us -> 356 us
  Pallas kernels: 372 us -> 350 us
    pallas_call x1, Pallas kernels: 372 us -> 350 us  [share_step(): pl.pallas_call(functools.partial(share_kernel, n), out_shape=jax.ShapeDty...]
where the time goes in v2:
time: 356 us
  Pallas kernels  350 us (98%)
  local copies, waits for them, and re-layouts  4.79 us (1%)
    pallas_call x1, Pallas kernels, share_step(): pl.pallas_call(functools.partial(share_kernel, n), out_shape=jax.ShapeDty...  350 us

profile of v2, /device:TPU:0, one launch (start us, length us, event | category | flops | bytes accessed | tf_op | source)
XLA Modules:
  0.0 356.0 jit_solution(13522975792552838681)
XLA Ops:
  1.3 349.9 %share_step.1 = f32[64,2,64,128]{3,2,1,0:T(8,128)} custom-call(f32[64,2,64,128]{3,2,1,0:T(8,128)} %start.1, f32[64,2,16,128]{3,2,1,0:T(8,128)} %guess.1, s32[1,256]{1,0:T(1,128)} %bitcast.6, f32[1,1]{1,0:T(1,128)} %bitcast.4.coupling, s32[1,4]{1,0:T(1,128)} %bitcast.7, s32[1,1]{1,0:T(1,128)} %bitcast.5.expiring), custom_call_target="tpu_custom_call" | custom-call | tf_op jit(solution)/shard_map/share_step/pallas_call | solution.py:1046
  351.2 4.8 %copy.10 = f32[64,2,64,128]{3,2,1,0:T(8,128)} copy(f32[64,2,64,128]{3,2,1,0:T(8,128)} %share_step.1) | data formatting | bytes 8388608

commit v3 on v2

--- a/solution.py
+++ b/solution.py
@@ -374,10 +374,13 @@
 
 
 SUBLANES = 8
-CHUNK = 2
+CHUNK = 1
 AHEAD = 3
-LAG = 3
-LEAD = (8, 4)
+LAG = 2
+LEAD = (4, 6)
+ARRIVE = 3
+LAST_AT = 11
+PANEL_AT = 6
 
 
 def block_transpose(blocks, lane, width):
@@ -396,8 +399,8 @@
 
 def share_kernel(
     n, start, guess, ordering, coupling, slab_owner, expiring,
-    out, snd, recv, sig, rx_g, rx_s, stk_a, stk_b, wvec, rbuf, lbuf, tot, guess_all, fwd_split, back_split,
-    fl, fs, fr, gl, gs, gr, sl, ss, sr, tl, ts, tr, rs, rr, ls, lr, credit, room,
+    result, out, out_sem, snd, recv, sig, rx_g, rx_s, stk_a, stk_b, wvec, rbuf, lbuf, tot, guess_all, fwd_split, back_split,
+    fs, fr, gs, gr, ss, sr, ts, tr, rs, rr, ls, lr, credit, room,
     al, aps, apr, axs, axr, aqs, aqr,
 ):
     mom, tm = lax.axis_index("mom"), lax.axis_index("tm")
@@ -454,25 +457,26 @@
 
     def forward(q, o):
         peer = lax.rem(mom + o, n)
-        return remote(snd.at[peer, span(q)], recv.at[span(q), :, mom], fs.at[q, o], fr.at[q, o], {"mom": peer})
+        return remote(snd.at[peer, span(q)], recv.at[span(q), :, mom], fs.at[o], fr.at[q], {"mom": peer})
 
     def forward_own(q):
-        return local(snd.at[mom, span(q)], recv.at[span(q), :, mom], fl.at[q])
+        return local(snd.at[mom, span(q)], recv.at[span(q), :, mom], fr.at[q])
 
     def panel_out(q, o):
         peer = lax.rem(tm + o, n)
-        return remote(recv.at[span(q), :, :, peer], rx_g.at[tm, span(q)], gs.at[q, o], gr.at[q, o], {"tm": peer})
+        return remote(recv.at[span(q), :, :, peer], rx_g.at[tm, span(q)], gs.at[o], gr.at[q // half_chunks], {"tm": peer})
 
     def panel_own(q):
-        return local(recv.at[span(q), :, :, tm], rx_g.at[tm, span(q)], gl.at[q])
+        return local(recv.at[span(q), :, :, tm], rx_g.at[tm, span(q)], gr.at[q // half_chunks])
 
     def sigma_out(n_pass, q, o):
         peer = lax.rem(tm + o, n)
         return remote(
-            sig.at[span(q), :, :, peer], rx_s.at[tm, span(q)], ss.at[n_pass, q, o], sr.at[n_pass, q, o], {"tm": peer})
+            sig.at[span(q), :, :, peer], rx_s.at[tm, span(q)], ss.at[n_pass, o], sr.at[n_pass, q // half_chunks],
+            {"tm": peer})
 
     def sigma_own(n_pass, q):
-        return local(sig.at[span(q), :, :, tm], rx_s.at[tm, span(q)], sl.at[n_pass, q])
+        return local(sig.at[span(q), :, :, tm], rx_s.at[tm, span(q)], sr.at[n_pass, q // half_chunks])
 
     def place(p):
         half, rest = p // per_half, p % per_half
@@ -486,27 +490,34 @@
         peer = lax.rem(tm + o, n)
         at, ks = pl.ds(half * SUBLANES, SUBLANES), pl.ds(sub * SUBLANES, SUBLANES)
         return remote(
-            snd.at[peer, at, s, block, ks], recv.at[at, s, block, tm, ks], ts.at[p, o], tr.at[p, o], {"tm": peer})
+            snd.at[peer, at, s, block, ks], recv.at[at, s, block, tm, ks], ts.at[o], tr.at[half], {"tm": peer})
 
     def next_own(p):
         half, sub, s, block = place(p)
         at, ks = pl.ds(half * SUBLANES, SUBLANES), pl.ds(sub * SUBLANES, SUBLANES)
-        return local(snd.at[tm, at, s, block, ks], recv.at[at, s, block, tm, ks], tl.at[p])
+        return local(snd.at[tm, at, s, block, ks], recv.at[at, s, block, tm, ks], tr.at[half])
 
     def window(p):
         half, sub, s, block = place(p)
         return pl.ds(block * quarter + sub * SUBLANES, SUBLANES), s, half
 
+    def whole(ref, sem):
+        return local(ref, ref, sem)
+
+    def sent(n_pass, p):
+        half, _, _, block = place(p)
+        return half if n_pass == 0 else block
+
     def right_out(n_pass, p):
         at = window(p)
         return remote(
-            rbuf.at[at], rbuf.at[at], rs.at[n_pass, p], rr.at[n_pass, p],
+            rbuf.at[at], rbuf.at[at], rs.at[n_pass, sent(n_pass, p)], rr.at[p],
             {"mom": jnp.minimum(mom + 1, n - 1)})
 
     def left_out(n_pass, p):
         at = window(p)
         return remote(
-            lbuf.at[at], lbuf.at[at], ls.at[n_pass, p], lr.at[n_pass, p],
+            lbuf.at[at], lbuf.at[at], ls.at[n_pass, sent(n_pass, p)], lr.at[p],
             {"mom": jnp.maximum(mom - 1, 0)})
 
     class Spread:
@@ -522,11 +533,11 @@
         def across(self, o):
             peer = lax.rem(tm_x + o, n_x)
             return remote(
-                self.source, self.target(tm), axs.at[self.at, o], axr.at[self.at, o], {"tm": peer * 2 + core})
+                self.source, self.target(tm), axs.at[self.at, o - 1], axr.at[self.at, o - 1], {"tm": peer * 2 + core})
 
         def relay(self, o):
             held = self.target(lax.rem(tm_x + n_x - o, n_x) * 2 + core)
-            return remote(held, held, aqs.at[self.at, o], aqr.at[self.at, o], partner)
+            return remote(held, held, aqs.at[self.at, o - 1], aqr.at[self.at, o - 1], partner)
 
         def begin(self):
             for o in range(1, n_x):
@@ -552,13 +563,14 @@
                 self.across(o).wait_send()
 
     guesses = Spread(0, guess, lambda t: guess_all.at[t])
-    firsts = [
-        Spread(1 + half, tot.at[0, :, :, half], lambda t, half=half: own_first.at[pl.ds(t * quarter, quarter), :, half])
-        for half in range(halves)]
+    def firsts(half, sub, s):
+        return Spread(
+            1 + (half * subs + sub) * SPIN + s, tot.at[0, pl.ds(sub * SUBLANES, SUBLANES), s, half],
+            lambda t: own_first.at[pl.ds(t * quarter + sub * SUBLANES, SUBLANES), s, half])
 
     def lasts(half, sub, s):
         return Spread(
-            1 + halves + (half * subs + sub) * SPIN + s, tot.at[1, pl.ds(sub * SUBLANES, SUBLANES), s, half],
+            1 + ((halves + half) * subs + sub) * SPIN + s, tot.at[1, pl.ds(sub * SUBLANES, SUBLANES), s, half],
             lambda t: own_last.at[half, pl.ds(t * quarter + sub * SUBLANES, SUBLANES), s])
 
     def spread_rows(target, half, s, k, parts):
@@ -589,12 +601,7 @@
         return tuple(stacks[n_pass][k, s, at].reshape(2 * PANEL, LANES) for at in range(2))
 
     def first_stack(half):
-        @pl.loop(0, half_chunks)
-        def _(d):
-            q = half * half_chunks + d
-            for o in range(1, n):
-                panel_out(q, o).wait_recv()
-            panel_own(q).wait()
+        whole(rx_g.at[:, pl.ds(half * SUBLANES, SUBLANES)], gr.at[half]).wait()
 
         @pl.loop(0, local_k, unroll=4)
         def _(k):
@@ -638,27 +645,15 @@
         sigma_own(n_pass, q).start()
 
     def wait_sigma(n_pass, half):
-        @pl.loop(0, half_chunks)
-        def _(d):
-            q = half * half_chunks + d
-            for o in range(1, n):
-                sigma_out(n_pass, q, o).wait_recv()
-            sigma_own(n_pass, q).wait()
+        whole(rx_s.at[:, pl.ds(half * SUBLANES, SUBLANES)], sr.at[n_pass, half]).wait()
 
     def second_sigma(q):
         half = q // half_chunks
 
         @pl.when(q % half_chunks == 0)
         def _():
-            @pl.loop(0, per_half)
-            def _(d):
-                p = half * per_half + d
-                for o in range(1, n):
-                    next_out(p, o).wait_recv()
-                next_own(p).wait()
-
-        for o in range(1, n):
-            sigma_out(0, q, o).wait_send()
+            whole(recv.at[pl.ds(half * SUBLANES, SUBLANES)], tr.at[half]).wait()
+
         sigma(q)
         send_sigma(1, q)
 
@@ -768,6 +763,10 @@
         @pl.when(block == mom)
         def _():
             each(p, lambda at, m: [(tot, (0, m) + at[1:], part[at])])
+
+            @pl.when(half < halves - 1)
+            def _():
+                firsts(half, sub, s).begin()
 
         results = []
         for m in range(SUBLANES):
@@ -794,8 +793,16 @@
         for k, s, new in results:
             own_first[k, s] = new.reshape(halves, half_rows, LANES)
 
+    def store(sub, s):
+        parts = (n, quarter, SPIN, PANEL, LANES)
+        at = pl.ds(sub * SUBLANES, SUBLANES)
+        return local(
+            out.reshape(parts).at[:, at, s], result.reshape(parts).at[:, at, s], out_sem.at[sub * SPIN + s])
+
     def finish(sub, s):
         is_block = chosen > 0.5
+        for half in range(halves):
+            lasts(half, sub, s).pass_on()
         for half in range(halves):
             lasts(half, sub, s).arrive()
 
@@ -814,6 +821,8 @@
             for k, new in results:
                 out[k, s] = new
 
+        store(sub, s).start()
+
     def begin_forward(q):
         for o in range(1, n):
             forward(q, o).start()
@@ -839,8 +848,8 @@
     owner_expiring = jnp.sum(jnp.where(slabs == oldest, owners, 0.0), axis=1, keepdims=True)
     position = slab_mine - oldest
     position = jnp.where(position < 0.0, position + n, position)
-    within = (mom * rows + lane % rows).astype(jnp.float32)
-    ahead = (n * PANEL - 1) - (position * PANEL + within)
+    held = (mom * rows + lane % rows).astype(jnp.float32)
+    ahead = (n * PANEL - 1) - (position * PANEL + held)
     strength = coupling[...] * coupling[...]
     wvec[...] = strength * (jnp.exp(-1.5 * ahead / (n * PANEL)) / math.sqrt(n * PANEL))
     chosen = jnp.where(owner_expiring == mine, jnp.ones((1, LANES), jnp.float32), 0.0)
@@ -849,9 +858,7 @@
     def _(q):
         @pl.when(q < chunks)
         def _():
-            for o in range(1, n):
-                forward(q, o).wait_recv()
-            forward_own(q).wait()
+            whole(recv.at[span(q)], fr.at[q]).wait()
 
             @pl.when(q + AHEAD < chunks)
             def _():
@@ -872,34 +879,95 @@
         def _():
             first_stack(halves - 1)
 
-    @pl.loop(0, chunks)
-    def _(q):
-        for o in range(1, n):
-            forward(q, o).wait_send()
-            panel_out(q, o).wait_send()
+    for o in range(1, n):
+        whole(snd.at[0], fs.at[o]).wait()
+        whole(recv.at[:, :, :, 0], gs.at[o]).wait()
+        whole(sig.at[:, :, :, 0], ss.at[0, o]).wait()
 
     for o in range(1, n):
         pl.semaphore_signal(room, inc=1, device_id={"tm": lax.rem(tm + o, n)}, device_id_type=MESH)
     guesses.begin()
 
-    lead = LEAD[0]
-    told = per_half + lead + LAG
-    sigma_at = told + 3
-
-    @pl.loop(0, pieces + lead + LAG)
+    def within(low, x, high):
+        return (x >= low) & (x < high)
+
+    lead, rest = LEAD[0], LEAD[1] + LAG
+    told = lead + LAG
+    first_sigma_at = told + per_half + ARRIVE
+    last_sigma_at = told + pieces + 1
+    last_at = told + per_half + ARRIVE + LAST_AT
+    panel_at = last_at + (halves - 1) * (per_half + rest) + PANEL_AT
+    period = per_half + rest
+
+    def last_piece(u, body):
+        seg, at = u // period, u % period
+
+        @pl.when((u >= 0) & (seg < halves) & (at < per_half))
+        def _():
+            body(seg * per_half + at)
+
+    def last_start(p):
+        for half in range(halves):
+            @pl.when(p == half * per_half)
+            def _():
+                @pl.when(mom > 0)
+                def _():
+                    pl.semaphore_wait(credit.at[half, 0], 1)
+
+                @pl.when(mom < n - 1)
+                def _():
+                    pl.semaphore_wait(credit.at[half, 1], 1)
+
+        convolve(1, p)
+        origin(1, p)
+
+    def last_far(p):
+        far_step(1, p)
+        half, sub, s, block = place(p)
+
+        @pl.when(block == mom)
+        def _():
+            lasts(half, sub, s).begin()
+
+        d = p - pieces + 2 * (subs * SPIN - 1)
+
+        @pl.when((d >= 0) & (d % 2 == 0))
+        def _():
+            finish((d // 2) // SPIN, (d // 2) % SPIN)
+
+    def free(half):
+        @pl.when(mom < n - 1)
+        def _():
+            whole(rbuf.at[:, :, half], rs.at[0, half]).wait()
+
+        @pl.when(mom > 0)
+        def _():
+            whole(lbuf.at[:, :, half], ls.at[0, half]).wait()
+
+        @pl.when(mom > 0)
+        def _():
+            pl.semaphore_signal(
+                credit.at[half, 1], inc=1, device_id={"mom": jnp.maximum(mom - 1, 0)}, device_id_type=MESH)
+
+        @pl.when(mom < n - 1)
+        def _():
+            pl.semaphore_signal(
+                credit.at[half, 0], inc=1, device_id={"mom": jnp.minimum(mom + 1, n - 1)}, device_id_type=MESH)
+
+    @pl.loop(0, last_at + halves * period)
     def _(t):
         @pl.when(t < pieces)
         def _():
             convolve(0, t)
             origin(0, t)
 
-        @pl.when((t >= lead) & (t - lead < pieces))
+        @pl.when(within(lead, t, lead + pieces))
         def _():
             near_step(0, t - lead)
 
-        @pl.when(t >= lead + LAG)
-        def _():
-            p = t - lead - LAG
+        @pl.when(within(told, t, told + pieces))
+        def _():
+            p = t - told
             far_step(0, p)
 
             @pl.when(p == 0)
@@ -908,125 +976,79 @@
 
             update(p)
 
-        for half in range(halves - 1):
-            @pl.when(t == told + half * per_half)
+        for half in range(halves):
+            @pl.when(t == told + (half + 1) * per_half + ARRIVE + 1)
             def _():
-                firsts[half].begin()
-
-        @pl.when(t == told)
+                free(half)
+
+        @pl.when(t == told + per_half)
         def _():
             guesses.pass_on()
 
-        d = t - sigma_at
-
-        @pl.when((d >= 0) & (d < 2 * (halves - 1) * half_chunks) & (d % 2 == 0))
-        def _():
-            second_sigma(d // 2)
-
-    @pl.loop(0, pieces)
-    def _(p):
-        @pl.when(mom < n - 1)
-        def _():
-            right_out(0, p).wait_send()
-
-        @pl.when(mom > 0)
-        def _():
-            left_out(0, p).wait_send()
-
-    @pl.when(mom > 0)
-    def _():
-        pl.semaphore_signal(credit.at[1], inc=1, device_id={"mom": jnp.maximum(mom - 1, 0)}, device_id_type=MESH)
-
-    @pl.when(mom < n - 1)
-    def _():
-        pl.semaphore_signal(credit.at[0], inc=1, device_id={"mom": jnp.minimum(mom + 1, n - 1)}, device_id_type=MESH)
-
-    @pl.when(mom > 0)
-    def _():
-        pl.semaphore_wait(credit.at[0], 1)
-
-    @pl.when(mom < n - 1)
-    def _():
-        pl.semaphore_wait(credit.at[1], 1)
-
-    lead = LEAD[1]
-    panel_at = 2 * per_half - 2 * local_k // SUBLANES + 6
-
-    @pl.loop(0, pieces + lead + LAG)
-    def _(t):
-        @pl.when(t < pieces)
-        def _():
-            convolve(1, t)
-            origin(1, t)
-
-        @pl.when((t >= 4) & (t < 4 + 2 * half_chunks) & (t % 2 == 0))
-        def _():
-            second_sigma((halves - 1) * half_chunks + (t - 4) // 2)
-
-        @pl.when((t >= lead) & (t - lead < pieces))
-        def _():
-            near_step(1, t - lead)
-
-        @pl.when(t >= lead + LAG)
-        def _():
-            p = t - lead - LAG
-            far_step(1, p)
-            half, sub, s, block = place(p)
-
-            @pl.when(block == mom)
-            def _():
-                lasts(half, sub, s).begin()
-
-        @pl.when(t == 4 + 2 * half_chunks)
-        def _():
-            firsts[halves - 1].begin()
+        @pl.when(within(first_sigma_at, t, first_sigma_at + (halves - 1) * half_chunks))
+        def _():
+            second_sigma(t - first_sigma_at)
+
+        last_piece(t - last_at, last_start)
+        last_piece(t - last_at - LEAD[1], lambda p: near_step(1, p))
+        last_piece(t - last_at - rest, last_far)
+
+        @pl.when(within(last_sigma_at + ARRIVE - 1, t, last_sigma_at + ARRIVE + 1))
+        def _():
+            @pl.loop(0, half_chunks // 2)
+            def _(d):
+                second_sigma((halves - 1) * half_chunks + (t - last_sigma_at - ARRIVE + 1) * (half_chunks // 2) + d)
+
+        @pl.when(t == last_sigma_at + ARRIVE + 1)
+        def _():
+            @pl.loop(0, subs * SPIN)
+            def _(d):
+                firsts(halves - 1, d // SPIN, d % SPIN).begin()
 
         @pl.when(t == panel_at)
         def _():
-            for first in firsts:
-                first.pass_on()
-            for first in firsts:
-                first.arrive()
-
-        @pl.when((t >= panel_at) & (t < panel_at + 2 * local_k // SUBLANES))
-        def _():
-            own_panel(t - panel_at)
-
-    guesses.arrive()
-
-    @pl.loop(0, subs * SPIN)
+            @pl.loop(0, halves * subs * SPIN)
+            def _(d):
+                firsts(d // (subs * SPIN), d // SPIN % subs, d % SPIN).pass_on()
+
+            @pl.loop(0, halves * subs * SPIN)
+            def _(d):
+                firsts(d // (subs * SPIN), d // SPIN % subs, d % SPIN).arrive()
+
+            guesses.arrive()
+
+        @pl.when(within(panel_at, t, panel_at + local_k // SUBLANES))
+        def _():
+            own_panel(2 * (t - panel_at))
+            own_panel(2 * (t - panel_at) + 1)
+
+    finish(subs - 1, SPIN - 1)
+
+    for block in range(n):
+        ks = pl.ds(block * quarter, quarter)
+
+        @pl.when((mom < n - 1) & (block > mom))
+        def _():
+            whole(rbuf.at[ks], rs.at[1, block]).wait()
+
+        @pl.when((mom > 0) & (block < mom))
+        def _():
+            whole(lbuf.at[ks], ls.at[1, block]).wait()
+
+    for o in range(1, n):
+        whole(snd.at[0], ts.at[o]).wait()
+        whole(sig.at[:, :, :, 0], ss.at[1, o]).wait()
+
+    @pl.loop(0, halves * subs * SPIN)
     def _(d):
-        for half in range(halves):
-            lasts(half, d // SPIN, d % SPIN).pass_on()
-        finish(d // SPIN, d % SPIN)
-
-    @pl.loop(0, pieces)
-    def _(p):
-        _, send_right, _, send_left, _ = flows(1, p)
-
-        @pl.when((mom < n - 1) & send_right)
-        def _():
-            right_out(1, p).wait_send()
-
-        @pl.when((mom > 0) & send_left)
-        def _():
-            left_out(1, p).wait_send()
-
-        for o in range(1, n):
-            next_out(p, o).wait_send()
-
-    @pl.loop(0, chunks)
-    def _(q):
-        for o in range(1, n):
-            sigma_out(1, q, o).wait_send()
-
-    for half in range(halves):
-        @pl.loop(0, subs * SPIN)
-        def _(d):
-            lasts(half, d // SPIN, d % SPIN).end()
+        at = d // (subs * SPIN), d // SPIN % subs, d % SPIN
+        firsts(*at).end()
+        lasts(*at).end()
+
     guesses.end()
-    for first in firsts:
-        first.end()
+    for sub in range(subs):
+        for s in range(SPIN):
+            store(sub, s).wait()
 
 
 def share_step(n, start, guess, ordering, coupling, slab_owner, expiring):
@@ -1034,7 +1056,7 @@
     quarter, rows = local_k // n, PANEL // n
     halves, subs = rows // SUBLANES, quarter // SUBLANES
     pieces, chunks = halves * n * subs * SPIN, rows // CHUNK
-    spreads = 1 + halves + halves * subs * SPIN
+    spreads, far = 1 + 2 * halves * subs * SPIN, max(n // 2 - 1, 1)
     half_rows = n * SUBLANES
     f32, bf16 = jnp.float32, jnp.bfloat16
     dma = pltpu.SemaphoreType.DMA
@@ -1047,8 +1069,9 @@
         functools.partial(share_kernel, n),
         out_shape=jax.ShapeDtypeStruct(start.shape, f32),
         in_specs=[vmem] * 6,
-        out_specs=vmem,
+        out_specs=pl.BlockSpec(memory_space=pl.ANY),
         scratch_shapes=[
+            pltpu.VMEM(start.shape, f32), dma((subs * SPIN,)),
             moved, grid, grid, moved, moved,
             stack, stack, pltpu.VMEM((1, LANES), f32),
             pltpu.VMEM(square, f32), pltpu.VMEM(square, f32),
@@ -1056,14 +1079,12 @@
             pltpu.VMEM((n,) + guess.shape, f32),
             pltpu.VMEM((2, 2 * K, K), bf16),
             pltpu.VMEM((2, K, 2 * K), bf16),
-            dma((chunks,)), dma((chunks, n)), dma((chunks, n)),
-            dma((chunks,)), dma((chunks, n)), dma((chunks, n)),
-            dma((PASSES, chunks)), dma((PASSES, chunks, n)), dma((PASSES, chunks, n)),
-            dma((pieces,)), dma((pieces, n)), dma((pieces, n)),
-            dma((PASSES, pieces)), dma((PASSES, pieces)), dma((PASSES, pieces)), dma((PASSES, pieces)),
-            pltpu.SemaphoreType.REGULAR((2,)), pltpu.SemaphoreType.REGULAR,
+            dma((n,)), dma((chunks,)), dma((n,)), dma((halves,)),
+            dma((PASSES, n)), dma((PASSES, halves)), dma((n,)), dma((halves,)),
+            dma((PASSES, max(n, halves))), dma((pieces,)), dma((PASSES, max(n, halves))), dma((pieces,)),
+            pltpu.SemaphoreType.REGULAR((halves, 2)), pltpu.SemaphoreType.REGULAR,
             dma((spreads,)), dma((spreads,)), dma((spreads,)),
-            dma((spreads, n)), dma((spreads, n)), dma((spreads, n)), dma((spreads, n)),
+            dma((spreads, far)), dma((spreads, far)), dma((spreads, far)), dma((spreads, far)),
         ],
         compiler_params=pltpu.CompilerParams(
             collective_id=0, has_side_effects=True, vmem_limit_bytes=63 * 1024 * 1024),

time: 356 us -> 332 us (0.933)
  Pallas kernels: 350 us -> 325 us
    pallas_call x1, Pallas kernels: 350 us -> 325 us  [share_step(): pl.pallas_call(functools.partial(share_kernel, n), out_shape=jax.ShapeDty...]
where the time goes in v3:
time: 332 us
  Pallas kernels  325 us (98%)
  local copies, waits for them, and re-layouts  4.79 us (1%)
    pallas_call x1, Pallas kernels, share_step(): pl.pallas_call(functools.partial(share_kernel, n), out_shape=jax.ShapeDty...  325 us

profile of v3, /device:TPU:0, one launch (start us, length us, event | category | flops | bytes accessed | tf_op | source)
XLA Modules:
  0.0 331.6 jit_solution(15247661141586562235)
XLA Ops:
  1.3 325.5 %share_step.1 = f32[64,2,64,128]{3,2,1,0:T(8,128)} custom-call(f32[64,2,64,128]{3,2,1,0:T(8,128)} %start.1, f32[64,2,16,128]{3,2,1,0:T(8,128)} %guess.1, s32[1,256]{1,0:T(1,128)} %bitcast.6, f32[1,1]{1,0:T(1,128)} %bitcast.4.coupling, s32[1,4]{1,0:T(1,128)} %bitcast.7, s32[1,1]{1,0:T(1,128)} %bitcast.5.expiring), custom_call_target="tpu_custom_call" | custom-call | tf_op jit(solution)/shard_map/share_step/pallas_call | solution.py:1068
  326.8 4.8 %copy.10 = f32[64,2,64,128]{3,2,1,0:T(8,128)} copy(f32[64,2,64,128]{3,2,1,0:T(8,128)} %share_step.1) | data formatting | bytes 8388608

commit v4 on v3

--- a/solution.py
+++ b/solution.py
@@ -375,12 +375,24 @@
 
 SUBLANES = 8
 CHUNK = 1
-AHEAD = 3
+AHEAD = 2
 LAG = 2
-LEAD = (4, 6)
-ARRIVE = 3
-LAST_AT = 11
+LEAD = (4, 7)
+ARRIVE = 1
+FINISH_AT = 7
+BURST = 4
+SIGMA_AT = 3
+LAST_AT = 12
 PANEL_AT = 6
+
+
+def wide(left, right, transposed=False):
+    rows = left[0].shape[0]
+    dims = (((1,), (1 if transposed else 0,)), ((), ()))
+    both = lax.dot_general(
+        jnp.concatenate(left, axis=0), jnp.concatenate(right, axis=0 if transposed else 1), dims,
+        preferred_element_type=jnp.float32)
+    return both[:rows, :LANES] + (both[:rows, LANES:] + both[rows:, :LANES])
 
 
 def block_transpose(blocks, lane, width):
@@ -668,7 +680,7 @@
         for m in range(SUBLANES):
             k = block * quarter + sub * SUBLANES + m
             value = split(gather_rows(flat_rx_s, half, s, k))
-            results.append((k, dot3(value, stack_of(n_pass, k, s), True)))
+            results.append((k, wide(value, stack_of(n_pass, k, s), True)))
         for k, result in results:
             part[k, s, half] = result
 
@@ -772,7 +784,7 @@
         for m in range(SUBLANES):
             k = block * quarter + sub * SUBLANES + m
             old = stk_a[k, s, 0, 0, half].astype(jnp.float32) + stk_a[k, s, 1, 0, half].astype(jnp.float32)
-            results.append((k, old + step_scale * dot3(split(part[k, s, half]), stack_of(0, k, s))))
+            results.append((k, old + step_scale * wide(split(part[k, s, half]), stack_of(0, k, s))))
         for k, new in results:
             keep_stack(1, k, s, half, new)
             spread_rows(flat_snd, half, s, k, [new[g * SUBLANES:(g + 1) * SUBLANES, :] for g in range(n)])
@@ -788,7 +800,7 @@
             for s in range(SPIN):
                 first = start[k, s]
                 right = split(jnp.concatenate([first, rot(first)], axis=0))
-                new = first + step_scale * dot3(split(own_first[k, s].reshape(PANEL, LANES)), right)
+                new = first + step_scale * wide(split(own_first[k, s].reshape(PANEL, LANES)), right)
                 results.append((k, s, new))
         for k, s, new in results:
             own_first[k, s] = new.reshape(halves, half_rows, LANES)
@@ -799,29 +811,33 @@
         return local(
             out.reshape(parts).at[:, at, s], result.reshape(parts).at[:, at, s], out_sem.at[sub * SPIN + s])
 
-    def finish(sub, s):
+    def finish(d):
+        sub, s, t = d // n // SPIN, d // n % SPIN, d % n
         is_block = chosen > 0.5
-        for half in range(halves):
-            lasts(half, sub, s).pass_on()
-        for half in range(halves):
-            lasts(half, sub, s).arrive()
-
-        @pl.loop(0, n)
-        def _(t):
-            results = []
-            for m in range(SUBLANES):
-                k = t * quarter + sub * SUBLANES + m
-                whole = jnp.concatenate([own_last[half, k, s] for half in range(halves)], axis=0)
-                d_rows = jnp.concatenate([guess_all[at, k, s] for at in range(n)], axis=0)
-                right = jnp.where(is_block, whole, own_first[k, s].reshape(PANEL, LANES))
-                left = jnp.where(is_block, d_rows, whole)
-                right = split(jnp.concatenate([right, rot(right)], axis=0))
-                new = jnp.where(is_block, d_rows, start[k, s]) + step_scale * dot3(split(left), right)
-                results.append((k, new))
-            for k, new in results:
-                out[k, s] = new
-
-        store(sub, s).start()
+
+        @pl.when(t == 0)
+        def _():
+            for half in range(halves):
+                lasts(half, sub, s).pass_on()
+            for half in range(halves):
+                lasts(half, sub, s).arrive()
+
+        results = []
+        for m in range(SUBLANES):
+            k = t * quarter + sub * SUBLANES + m
+            whole = jnp.concatenate([own_last[half, k, s] for half in range(halves)], axis=0)
+            d_rows = jnp.concatenate([guess_all[at, k, s] for at in range(n)], axis=0)
+            right = jnp.where(is_block, whole, own_first[k, s].reshape(PANEL, LANES))
+            left = jnp.where(is_block, d_rows, whole)
+            right = split(jnp.concatenate([right, rot(right)], axis=0))
+            new = jnp.where(is_block, d_rows, start[k, s]) + step_scale * wide(split(left), right)
+            results.append((k, new))
+        for k, new in results:
+            out[k, s] = new
+
+        @pl.when(t == n - 1)
+        def _():
+            store(sub, s).start()
 
     def begin_forward(q):
         for o in range(1, n):
@@ -894,7 +910,7 @@
     lead, rest = LEAD[0], LEAD[1] + LAG
     told = lead + LAG
     first_sigma_at = told + per_half + ARRIVE
-    last_sigma_at = told + pieces + 1
+    last_sigma_at = told + pieces + SIGMA_AT
     last_at = told + per_half + ARRIVE + LAST_AT
     panel_at = last_at + (halves - 1) * (per_half + rest) + PANEL_AT
     period = per_half + rest
@@ -929,11 +945,11 @@
         def _():
             lasts(half, sub, s).begin()
 
-        d = p - pieces + 2 * (subs * SPIN - 1)
-
-        @pl.when((d >= 0) & (d % 2 == 0))
-        def _():
-            finish((d // 2) // SPIN, (d // 2) % SPIN)
+        d = p - (pieces - per_half) - FINISH_AT
+
+        @pl.when(d >= 0)
+        def _():
+            finish(d)
 
     def free(half):
         @pl.when(mom < n - 1)
@@ -993,13 +1009,13 @@
         last_piece(t - last_at - LEAD[1], lambda p: near_step(1, p))
         last_piece(t - last_at - rest, last_far)
 
-        @pl.when(within(last_sigma_at + ARRIVE - 1, t, last_sigma_at + ARRIVE + 1))
-        def _():
-            @pl.loop(0, half_chunks // 2)
+        @pl.when(within(last_sigma_at, t, last_sigma_at + half_chunks // BURST))
+        def _():
+            @pl.loop(0, BURST)
             def _(d):
-                second_sigma((halves - 1) * half_chunks + (t - last_sigma_at - ARRIVE + 1) * (half_chunks // 2) + d)
-
-        @pl.when(t == last_sigma_at + ARRIVE + 1)
+                second_sigma((halves - 1) * half_chunks + (t - last_sigma_at) * BURST + d)
+
+        @pl.when(t == last_sigma_at + half_chunks // BURST)
         def _():
             @pl.loop(0, subs * SPIN)
             def _(d):
@@ -1022,7 +1038,9 @@
             own_panel(2 * (t - panel_at))
             own_panel(2 * (t - panel_at) + 1)
 
-    finish(subs - 1, SPIN - 1)
+    @pl.loop(per_half - FINISH_AT, per_half)
+    def _(d):
+        finish(d)
 
     for block in range(n):
         ks = pl.ds(block * quarter, quarter)

time: 332 us -> 320 us (0.964)
  Pallas kernels: 325 us -> 314 us
    pallas_call x1, Pallas kernels: 325 us -> 314 us  [share_step(): pl.pallas_call(functools.partial(share_kernel, n), out_shape=jax.ShapeDty...]
where the time goes in v4:
time: 320 us
  Pallas kernels  314 us (98%)
  local copies, waits for them, and re-layouts  4.79 us (1%)
    pallas_call x1, Pallas kernels, share_step(): pl.pallas_call(functools.partial(share_kernel, n), out_shape=jax.ShapeDty...  314 us

profile of v4, /device:TPU:0, one launch (start us, length us, event | category | flops | bytes accessed | tf_op | source)
XLA Modules:
  0.0 320.0 jit_solution(9923489310471809152)
XLA Ops:
  1.3 313.9 %share_step.1 = f32[64,2,64,128]{3,2,1,0:T(8,128)} custom-call(f32[64,2,64,128]{3,2,1,0:T(8,128)} %start.1, f32[64,2,16,128]{3,2,1,0:T(8,128)} %guess.1, s32[1,256]{1,0:T(1,128)} %bitcast.6, f32[1,1]{1,0:T(1,128)} %bitcast.4.coupling, s32[1,4]{1,0:T(1,128)} %bitcast.7, s32[1,1]{1,0:T(1,128)} %bitcast.5.expiring), custom_call_target="tpu_custom_call" | custom-call | tf_op jit(solution)/shard_map/share_step/pallas_call | solution.py:1086
  315.2 4.8 %copy.10 = f32[64,2,64,128]{3,2,1,0:T(8,128)} copy(f32[64,2,64,128]{3,2,1,0:T(8,128)} %share_step.1) | data formatting | bytes 8388608

commit v5 on v4

--- a/solution.py
+++ b/solution.py
@@ -662,6 +662,11 @@
     def second_sigma(q):
         half = q // half_chunks
 
+        @pl.when(q == 0)
+        def _():
+            for o in range(1, n):
+                whole(sig.at[:, :, :, 0], ss.at[0, o]).wait()
+
         @pl.when(q % half_chunks == 0)
         def _():
             whole(recv.at[pl.ds(half * SUBLANES, SUBLANES)], tr.at[half]).wait()
@@ -898,7 +903,6 @@
     for o in range(1, n):
         whole(snd.at[0], fs.at[o]).wait()
         whole(recv.at[:, :, :, 0], gs.at[o]).wait()
-        whole(sig.at[:, :, :, 0], ss.at[0, o]).wait()
 
     for o in range(1, n):
         pl.semaphore_signal(room, inc=1, device_id={"tm": lax.rem(tm + o, n)}, device_id_type=MESH)

time: 320 us -> 320 us (level)
  no operation moved by 1% of the time
where the time goes in v5:
time: 320 us
  Pallas kernels  314 us (98%)
  local copies, waits for them, and re-layouts  4.79 us (1%)
    pallas_call x1, Pallas kernels, share_step(): pl.pallas_call(functools.partial(share_kernel, n), out_shape=jax.ShapeDty...  314 us

profile of v5, /device:TPU:0, one launch (start us, length us, event | category | flops | bytes accessed | tf_op | source)
XLA Modules:
  0.0 320.0 jit_solution(14687810684810129841)
XLA Ops:
  1.3 313.9 %share_step.1 = f32[64,2,64,128]{3,2,1,0:T(8,128)} custom-call(f32[64,2,64,128]{3,2,1,0:T(8,128)} %start.1, f32[64,2,16,128]{3,2,1,0:T(8,128)} %guess.1, s32[1,256]{1,0:T(1,128)} %bitcast.6, f32[1,1]{1,0:T(1,128)} %bitcast.4.coupling, s32[1,4]{1,0:T(1,128)} %bitcast.7, s32[1,1]{1,0:T(1,128)} %bitcast.5.expiring), custom_call_target="tpu_custom_call" | custom-call | tf_op jit(solution)/shard_map/share_step/pallas_call | solution.py:1090
  315.2 4.8 %copy.10 = f32[64,2,64,128]{3,2,1,0:T(8,128)} copy(f32[64,2,64,128]{3,2,1,0:T(8,128)} %share_step.1) | data formatting | bytes 8388608

commit v6 on v5

--- a/solution.py
+++ b/solution.py
@@ -598,7 +598,7 @@
         return jnp.concatenate(block_transpose(parts, lane, width), axis=0)
 
     def first_layout(half):
-        @pl.loop(0, local_k, unroll=4)
+        @pl.loop(0, local_k, unroll=8)
         def _(k):
             for s in range(SPIN):
                 parts = [start[k, s, half * half_rows + g * SUBLANES:half * half_rows + (g + 1) * SUBLANES, :]
@@ -1090,7 +1090,7 @@
     return pl.pallas_call(
         functools.partial(share_kernel, n),
         out_shape=jax.ShapeDtypeStruct(start.shape, f32),
-        in_specs=[vmem] * 6,
+        in_specs=[vmem, pl.BlockSpec(memory_space=pl.ANY)] + [vmem] * 4,
         out_specs=pl.BlockSpec(memory_space=pl.ANY),
         scratch_shapes=[
             pltpu.VMEM(start.shape, f32), dma((subs * SPIN,)),

time: 320 us -> 316 us (0.988)
  Pallas kernels: 314 us -> 310 us
    pallas_call x1, Pallas kernels: 314 us -> 310 us  [share_step(): pl.pallas_call(functools.partial(share_kernel, n), out_shape=jax.ShapeDty...]
where the time goes in v6:
time: 316 us
  Pallas kernels  310 us (98%)
  local copies, waits for them, and re-layouts  4.79 us (2%)
    pallas_call x1, Pallas kernels, share_step(): pl.pallas_call(functools.partial(share_kernel, n), out_shape=jax.ShapeDty...  310 us

profile of v6, /device:TPU:0, one launch (start us, length us, event | category | flops | bytes accessed | tf_op | source)
XLA Modules:
  0.0 316.3 jit_solution(10455070905604893238)
XLA Ops:
  1.3 310.2 %share_step.1 = f32[64,2,64,128]{3,2,1,0:T(8,128)} custom-call(f32[64,2,64,128]{3,2,1,0:T(8,128)} %start.1, f32[64,2,16,128]{3,2,1,0:T(8,128)} %guess.1, s32[1,256]{1,0:T(1,128)} %bitcast.6, f32[1,1]{1,0:T(1,128)} %bitcast.4.coupling, s32[1,4]{1,0:T(1,128)} %bitcast.7, s32[1,1]{1,0:T(1,128)} %bitcast.5.expiring), custom_call_target="tpu_custom_call" | custom-call | tf_op jit(solution)/shard_map/share_step/pallas_call | solution.py:1090
  311.5 4.8 %copy.10 = f32[64,2,64,128]{3,2,1,0:T(8,128)} copy(f32[64,2,64,128]{3,2,1,0:T(8,128)} %share_step.1) | data formatting | bytes 8388608

commit v7 on v6

--- a/solution.py
+++ b/solution.py
@@ -615,7 +615,7 @@
     def first_stack(half):
         whole(rx_g.at[:, pl.ds(half * SUBLANES, SUBLANES)], gr.at[half]).wait()
 
-        @pl.loop(0, local_k, unroll=4)
+        @pl.loop(0, local_k, unroll=8)
         def _(k):
             for s in range(SPIN):
                 keep_stack(0, k, s, half, gather_rows(flat_rx_g, half, s, k))

time: 316 us -> 314 us (level)
  no operation moved by 1% of the time
where the time goes in v7:
time: 314 us
  Pallas kernels  308 us (98%)
  local copies, waits for them, and re-layouts  4.79 us (2%)
    pallas_call x1, Pallas kernels, share_step(): pl.pallas_call(functools.partial(share_kernel, n), out_shape=jax.ShapeDty...  308 us

profile of v7, /device:TPU:0, one launch (start us, length us, event | category | flops | bytes accessed | tf_op | source)
XLA Modules:
  0.0 314.2 jit_solution(9109261864690815648)
XLA Ops:
  1.3 308.1 %share_step.1 = f32[64,2,64,128]{3,2,1,0:T(8,128)} custom-call(f32[64,2,64,128]{3,2,1,0:T(8,128)} %start.1, f32[64,2,16,128]{3,2,1,0:T(8,128)} %guess.1, s32[1,256]{1,0:T(1,128)} %bitcast.6, f32[1,1]{1,0:T(1,128)} %bitcast.4.coupling, s32[1,4]{1,0:T(1,128)} %bitcast.7, s32[1,1]{1,0:T(1,128)} %bitcast.5.expiring), custom_call_target="tpu_custom_call" | custom-call | tf_op jit(solution)/shard_map/share_step/pallas_call | solution.py:1090
  309.4 4.8 %copy.10 = f32[64,2,64,128]{3,2,1,0:T(8,128)} copy(f32[64,2,64,128]{3,2,1,0:T(8,128)} %share_step.1) | data formatting | bytes 8388608
